TPU v7x, 32 devices: a whole 2x2x4 slice. The times are simulated.
32 devices in a mesh: gx: 4 (over z), gy: 4 (over y, core), gz: 2 (over x).
Axes of the slice: x: 2, y: 2, z: 4, core: 2. Of those that a mesh axis runs over, the one named last changes fastest.
Arguments:
- potential: float32 [64, 192, 256], P('gx', 'gy', 'gz'), may hold values from -6 to 6
- density_matrix: float32 [32, 169], P(('gx', 'gy', 'gz')), may hold values from -6 to 6
- delta_table: float32 [4, 9, 169], replicated, may hold values from -36 to 36
- coulomb: float32 [4, 169, 169], replicated, may hold values from -0.5 to 0.5
- radius: float32 [4], replicated, may hold values from 1.5 to 3
- atom_species: int32 [32], replicated, may hold values from 0 to 3
- slot_atom: int32 [32, 8], P(('gx', 'gy', 'gz')), may hold values from 0 to 31, as said below
- slot_corner: int32 [3, 32, 8], P(None, ('gx', 'gy', 'gz')), may hold values from -15 to 127, as said below
- slot_count: int32 [32], P(('gx', 'gy', 'gz')), may hold values from 1 to 8, as said below
- projections: float32 [32, 8, 13, 256], P(('gx', 'gy', 'gz')), may hold values from -1.5 to 1.5
Outputs:
- dh: float32 [32, 169], P(('gx', 'gy', 'gz'))
- applied: float32 [32, 8, 13, 256], P(('gx', 'gy', 'gz'))
Inputs may be any that keep to these rules, and one draw needn't show every extreme that they name: `slot_atom`: atom a is owned by domain a in row-major order over (gx, gy, gz). Its box of 16 cells a side lies inside the grid and its lowest cell lies in the owner's domain. The live slots of a domain name each atom whose box reaches the domain exactly once, in any order, and only those; the owner of such an atom has the domain's coordinates minus 0 or 1 along each axis. Dead slots hold 0. `slot_corner`: for a live slot, the atom's lowest box cell minus the domain's first cell, per axis; the same atom gives the same global corner in every domain. Dead slots hold 0. `slot_count`: live slots come first. Every domain lists the atom it owns, and some domain has all 8 slots live in every draw.
All inputs are finite; a program needn't handle non-finite values.
Results may differ from a plain program's by a relative error of at most 0.0003.
Values sent between devices are 32-bit elements; how exact they have to be, the bound alone decides.
No kernel may reach another device: no remote copies, remote signals or barrier semaphores. Data moves between devices by JAX's collectives and lax.ppermute only.
A program may use at most 64 MiB of HBM per device.

v0:
```python
import math

import jax
import jax.numpy as jnp
from jax import lax
from jax.sharding import PartitionSpec as P

BOX = 16
SHAPES = 9
NP = 13
SPECIES = 4


highest = lax.Precision.HIGHEST
harmonic_scale = 0.5 / math.sqrt(3.0)


def shifted(x, axis, by):
    devices = lax.axis_size(axis)
    pairs = [(i, i + by) for i in range(devices) if 0 <= i + by < devices]
    return lax.ppermute(x, axis, pairs)


def shape_table(radius):
    offsets = jnp.arange(BOX, dtype=jnp.float32) - (BOX - 1) / 2.0
    cube = (BOX, BOX, BOX)
    first = jnp.broadcast_to(offsets[:, None, None], cube).reshape(1, -1) / radius[:, None]
    second = jnp.broadcast_to(offsets[None, :, None], cube).reshape(1, -1) / radius[:, None]
    third = jnp.broadcast_to(offsets[None, None, :], cube).reshape(1, -1) / radius[:, None]
    square = first * first + second * second + third * third
    envelope = jnp.exp(-square)
    envelope = envelope / jnp.sum(envelope, axis=1, keepdims=True)
    harmonics = [
        jnp.ones_like(first),
        first,
        second,
        third,
        first * second,
        second * third,
        third * first,
        0.5 * (first * first - second * second),
        harmonic_scale * (3.0 * third * third - square),
    ]
    return jnp.stack([item * envelope for item in harmonics], axis=1)


def local(
    potential,
    density_matrix,
    delta_table,
    coulomb,
    radius,
    atom_species,
    slot_atom,
    slot_corner,
    slot_count,
    projections,
):
    size_y = lax.axis_size("gy")
    size_z = lax.axis_size("gz")
    index_x = lax.axis_index("gx")
    index_y = lax.axis_index("gy")
    index_z = lax.axis_index("gz")
    myself = (index_x * size_y + index_y) * size_z + index_z
    owned = density_matrix.shape[0]
    slots = slot_atom.shape[1]
    atoms = atom_species.shape[0]
    live = (jnp.arange(slots, dtype=jnp.int32) < slot_count[0]).astype(jnp.float32)
    atom_ids = slot_atom[0]
    corners = slot_corner[:, 0, :]
    margin = BOX - 1
    padded = jnp.pad(potential, ((margin, margin), (margin, margin), (margin, margin)))

    def cut_tile(corner_x, corner_y, corner_z):
        return lax.dynamic_slice(
            padded, (corner_x + margin, corner_y + margin, corner_z + margin), (BOX, BOX, BOX)
        ).reshape(-1)

    tiles = jax.vmap(cut_tile)(corners[0], corners[1], corners[2])
    table = shape_table(radius).reshape(SPECIES * SHAPES, BOX**3)
    values = jnp.dot(tiles, table.T, precision=highest)
    matches = atom_ids[:, None] == jnp.arange(atoms, dtype=jnp.int32)[None, :]
    slot_species = jnp.sum(jnp.where(matches, atom_species[None, :], 0), axis=1)
    partial_value = jnp.zeros((slots, SHAPES), jnp.float32)
    for kind in range(SPECIES):
        partial_value = (
            partial_value
            + (slot_species == kind).astype(jnp.float32)[:, None]
            * values[:, kind * SHAPES : (kind + 1) * SHAPES]
        )
    partial_value = partial_value * live[:, None]
    owner = atom_ids // owned
    owner_x = owner // (size_y * size_z)
    owner_y = owner // size_z % size_y
    owner_z = owner % size_z
    code = (
        (index_x - owner_x) * 4 + (index_y - owner_y) * 2 + (index_z - owner_z)
    ) * owned + atom_ids % owned
    code_hits = (code[:, None] == jnp.arange(8 * owned, dtype=jnp.int32)[None, :]).astype(
        jnp.float32
    )
    blocks = jnp.dot(code_hits.T, partial_value, precision=highest).reshape(2, 2, 2, owned, SHAPES)
    section = blocks[0] + shifted(blocks[1], "gx", -1)
    section = section[0] + shifted(section[1], "gy", -1)
    totals = section[0] + shifted(section[1], "gz", -1)
    own_species = lax.dynamic_slice_in_dim(atom_species, myself * owned, owned)
    dh_own = jnp.zeros((owned, NP * NP), jnp.float32)
    for kind in range(SPECIES):
        term = jnp.dot(totals, delta_table[kind], precision=highest) + 2.0 * jnp.dot(
            density_matrix, coulomb[kind].T, precision=highest
        )
        dh_own = dh_own + (own_species == kind).astype(jnp.float32)[:, None] * term
    along_x = jnp.stack([dh_own, shifted(dh_own, "gx", 1)])
    along_y = jnp.stack([along_x, shifted(along_x, "gy", 1)], axis=1)
    gathered = jnp.stack([along_y, shifted(along_y, "gz", 1)], axis=2)
    slot_dh = jnp.dot(code_hits, gathered.reshape(8 * owned, NP * NP), precision=highest)
    applied = (
        jnp.einsum(
            "sij,sib->sjb", slot_dh.reshape(slots, NP, NP), projections[0], precision=highest
        )
        * live[:, None, None]
    )
    return (dh_own, applied[None])


def solution(mesh):
    return jax.shard_map(
        local,
        mesh=mesh,
        in_specs=(
            P("gx", "gy", "gz"),
            P(("gx", "gy", "gz"), None),
            P(),
            P(),
            P(),
            P(),
            P(("gx", "gy", "gz"), None),
            P(None, ("gx", "gy", "gz"), None),
            P(("gx", "gy", "gz")),
            P(("gx", "gy", "gz"), None, None, None),
        ),
        out_specs=(P(("gx", "gy", "gz"), None), P(("gx", "gy", "gz"), None, None, None)),
        check_vma=False,
    )
```

profile of v0, /device:TPU:14, one launch (start us, length us, event | category | flops | bytes accessed | tf_op | source)
XLA Modules:
  0.0 71.7 jit_solution(7988757164023809421)
XLA Ops:
  0.7 0.7 %compare_select_fusion.2 = (s32[8,1]{0,1:T(1,128)S(1)}, s32[8,1]{0,1:T(1,128)S(1)}, s32[8,1]{0,1:T(1,128)S(1)}) fusion(s32[3,1,8]{2,1,0:T(1,128)} %param.17), kind=kLoop, calls=%fused_computation.71 | loop fusion | flops 96 | bytes 192 | tf_op jit(solution)/shard_map/vmap()/select_n | solution.py:75
  1.4 3.4 %pad.4 = f32[46,78,158]{2,1,0:T(8,128)} pad(f32[16,48,128]{2,1,0:T(8,128)} %param.10, f32[]{:T(128)} %constant.103.clone.1), padding=15_15x15_15x15_15 | pad | bytes 2660836 | tf_op jit(solution)/shard_map/jit(_pad)/pad | solution.py:72
  4.8 29.9 %while.1 = (s32[]{:T(128)}, f32[46,78,158]{2,1,0:T(8,128)}, s32[8,3]{0,1:T(4,128)S(1)}, f32[8,16,16,16]{3,2,1,0:T(8,128)S(1)}, s32[]{:T(128)}) while((s32[]{:T(128)}, f32[46,78,158]{2,1,0:T(8,128)}, s32[8,3]{0,1:T(4,128)S(1)}, f32[8,16,16,16]{3,2,1,0:T(8,128)S(1)}, s32[]{:T(128)}) %tuple.41), condition=%wide.while_cond, body=%wide.while_body.sunk | while | flops 2 | bytes 147593 | solution.py:75
  4.9 0.6 fusion.69
  5.5 3.1 %bitcast_dynamic-update-slice_fusion.2 = f32[8,16,16,16]{3,2,1,0:T(8,128)S(1)} fusion(f32[8,16,16,16]{3,2,1,0:T(8,128)S(1)} %get-tuple-element.86, s32[]{:T(128)S(6)} %copy.88, f32[46,78,158]{2,1,0:T(8,128)} %get-tuple-element.89, s32[]{:T(128)} %bitcast.139, s32[]{:T(128)} %bitcast.140, s32[]{:T(128)} %bitcast.141), kind=kLoop, calls=%fused_computation.clone.1 | loop fusion | bytes 147472 | tf_op jit(solution)/shard_map/vmap()/gather
  8.6 0.6 fusion.69
  9.2 3.1 %bitcast_dynamic-update-slice_fusion.2 = f32[8,16,16,16]{3,2,1,0:T(8,128)S(1)} fusion(f32[8,16,16,16]{3,2,1,0:T(8,128)S(1)} %get-tuple-element.86, s32[]{:T(128)S(6)} %copy.88, f32[46,78,158]{2,1,0:T(8,128)} %get-tuple-element.89, s32[]{:T(128)} %bitcast.139, s32[]{:T(128)} %bitcast.140, s32[]{:T(128)} %bitcast.141), kind=kLoop, calls=%fused_computation.clone.1 | loop fusion | bytes 147472 | tf_op jit(solution)/shard_map/vmap()/gather
  12.4 0.6 fusion.69
  13.0 3.1 %bitcast_dynamic-update-slice_fusion.2 = f32[8,16,16,16]{3,2,1,0:T(8,128)S(1)} fusion(f32[8,16,16,16]{3,2,1,0:T(8,128)S(1)} %get-tuple-element.86, s32[]{:T(128)S(6)} %copy.88, f32[46,78,158]{2,1,0:T(8,128)} %get-tuple-element.89, s32[]{:T(128)} %bitcast.139, s32[]{:T(128)} %bitcast.140, s32[]{:T(128)} %bitcast.141), kind=kLoop, calls=%fused_computation.clone.1 | loop fusion | bytes 147472 | tf_op jit(solution)/shard_map/vmap()/gather
  16.1 0.6 fusion.69
  16.7 3.1 %bitcast_dynamic-update-slice_fusion.2 = f32[8,16,16,16]{3,2,1,0:T(8,128)S(1)} fusion(f32[8,16,16,16]{3,2,1,0:T(8,128)S(1)} %get-tuple-element.86, s32[]{:T(128)S(6)} %copy.88, f32[46,78,158]{2,1,0:T(8,128)} %get-tuple-element.89, s32[]{:T(128)} %bitcast.139, s32[]{:T(128)} %bitcast.140, s32[]{:T(128)} %bitcast.141), kind=kLoop, calls=%fused_computation.clone.1 | loop fusion | bytes 147472 | tf_op jit(solution)/shard_map/vmap()/gather
  19.8 0.6 fusion.69
  20.4 3.1 %bitcast_dynamic-update-slice_fusion.2 = f32[8,16,16,16]{3,2,1,0:T(8,128)S(1)} fusion(f32[8,16,16,16]{3,2,1,0:T(8,128)S(1)} %get-tuple-element.86, s32[]{:T(128)S(6)} %copy.88, f32[46,78,158]{2,1,0:T(8,128)} %get-tuple-element.89, s32[]{:T(128)} %bitcast.139, s32[]{:T(128)} %bitcast.140, s32[]{:T(128)} %bitcast.141), kind=kLoop, calls=%fused_computation.clone.1 | loop fusion | bytes 147472 | tf_op jit(solution)/shard_map/vmap()/gather
  23.6 0.6 fusion.69
  24.2 3.1 %bitcast_dynamic-update-slice_fusion.2 = f32[8,16,16,16]{3,2,1,0:T(8,128)S(1)} fusion(f32[8,16,16,16]{3,2,1,0:T(8,128)S(1)} %get-tuple-element.86, s32[]{:T(128)S(6)} %copy.88, f32[46,78,158]{2,1,0:T(8,128)} %get-tuple-element.89, s32[]{:T(128)} %bitcast.139, s32[]{:T(128)} %bitcast.140, s32[]{:T(128)} %bitcast.141), kind=kLoop, calls=%fused_computation.clone.1 | loop fusion | bytes 147472 | tf_op jit(solution)/shard_map/vmap()/gather
  27.3 0.6 fusion.69
  27.9 3.1 %bitcast_dynamic-update-slice_fusion.2 = f32[8,16,16,16]{3,2,1,0:T(8,128)S(1)} fusion(f32[8,16,16,16]{3,2,1,0:T(8,128)S(1)} %get-tuple-element.86, s32[]{:T(128)S(6)} %copy.88, f32[46,78,158]{2,1,0:T(8,128)} %get-tuple-element.89, s32[]{:T(128)} %bitcast.139, s32[]{:T(128)} %bitcast.140, s32[]{:T(128)} %bitcast.141), kind=kLoop, calls=%fused_computation.clone.1 | loop fusion | bytes 147472 | tf_op jit(solution)/shard_map/vmap()/gather
  31.0 0.6 fusion.69
  31.6 3.1 %bitcast_dynamic-update-slice_fusion.2 = f32[8,16,16,16]{3,2,1,0:T(8,128)S(1)} fusion(f32[8,16,16,16]{3,2,1,0:T(8,128)S(1)} %get-tuple-element.86, s32[]{:T(128)S(6)} %copy.88, f32[46,78,158]{2,1,0:T(8,128)} %get-tuple-element.89, s32[]{:T(128)} %bitcast.139, s32[]{:T(128)} %bitcast.140, s32[]{:T(128)} %bitcast.141), kind=kLoop, calls=%fused_computation.clone.1 | loop fusion | bytes 147472 | tf_op jit(solution)/shard_map/vmap()/gather
  34.7 0.6 reshape.1709
  35.4 0.1 div.261
  35.6 0.1 div.258
  35.7 0.1 broadcast_in_dim.24
  35.8 0.1 div.254
  35.9 0.2 fusion.10
  36.1 0.1 constant_dynamic-update-slice_fusion
  36.3 0.2 multiply_dynamic-update-slice_fusion.6
  36.4 0.2 multiply_dynamic-update-slice_fusion.5
  36.6 0.2 multiply_dynamic-update-slice_fusion.4
  36.7 0.2 multiply_dynamic-update-slice_fusion.3
  36.9 0.2 multiply_dynamic-update-slice_fusion.2
  37.0 0.2 multiply_dynamic-update-slice_fusion.1
  37.2 0.2 multiply_dynamic-update-slice_fusion
  37.4 0.2 fusion.14
  37.5 0.4 copy.40
  37.9 0.1 reshape.1710
  38.6 0.6 fusion.63
  39.3 0.2 select_reduce_fusion
  39.5 0.3 fusion.22
  39.8 2.4 %collective-permute-start = (f32[2,2,1,9]{3,1,0,2:T(2,128)S(1)}, f32[2,2,1,9]{3,1,0,2:T(2,128)S(1)}, u32[]{:S(2)}, u32[]{:S(2)}) collective-permute-start(f32[2,2,1,9]{3,1,0,2:T(2,128)S(1)} %bitcast.163), channel_id=1, source_target_pairs={{8,0},{16,8},{24,16},{9,1},{17,9},{25,17},{10,2},{18,10},{26,18},{... | collective-permute-start | bytes 440 | tf_op jit(solution)/shard_map/ppermute | solution.py:21
  42.2 0.5 fusion.60
  42.7 0.2 fusion.1
  42.9 0.3 fusion.2
  43.2 0.3 fusion.3
  43.4 0.3 fusion.4
  43.7 0.6 dynamic_slice.3
  47.0 1.9 %collective-permute-start.1 = (f32[2,1,9]{2,0,1:T(2,128)S(1)}, f32[2,1,9]{2,0,1:T(2,128)S(1)}, u32[]{:S(2)}, u32[]{:S(2)}) collective-permute-start(f32[2,1,9]{2,0,1:T(2,128)S(1)} %slice_bitcast_fusion), channel_id=1, source_target_pairs={{2,0},{4,2},{6,4},{3,1},{5,3},{7,5},{10,8},{12,10},{14,12},{11,9},... | collective-permute-start | bytes 224 | tf_op jit(solution)/shard_map/ppermute | solution.py:21
  48.9 1.3 %collective-permute-done.1 = f32[2,1,9]{2,0,1:T(2,128)S(1)} collective-permute-done((f32[2,1,9]{2,0,1:T(2,128)S(1)}, f32[2,1,9]{2,0,1:T(2,128)S(1)}, u32[]{:S(2)}, u32[]{:S(2)}) %collective-permute-start.1) | collective-permute-done | bytes 104 | tf_op jit(solution)/shard_map/ppermute | solution.py:21
  50.2 2.4 %collective-permute-start.2 = (f32[1,9]{1,0:T(1,128)S(1)}, f32[1,9]{1,0:T(1,128)S(1)}, u32[]{:S(2)}, u32[]{:S(2)}) collective-permute-start(f32[1,9]{1,0:T(1,128)S(1)} %slice_bitcast_fusion.2), channel_id=1, source_target_pairs={{1,0},{3,2},{5,4},{7,6},{9,8},{11,10},{13,12},{15,14},{17,16},{19,... | collective-permute-start | bytes 116 | tf_op jit(solution)/shard_map/ppermute | solution.py:21
  52.6 1.3 %collective-permute-done.2 = f32[1,9]{1,0:T(1,128)S(1)} collective-permute-done((f32[1,9]{1,0:T(1,128)S(1)}, f32[1,9]{1,0:T(1,128)S(1)}, u32[]{:S(2)}, u32[]{:S(2)}) %collective-permute-start.2) | collective-permute-done | bytes 68 | tf_op jit(solution)/shard_map/ppermute | solution.py:21
  53.9 0.1 fusion.18
  54.0 0.1 fusion.19
  54.1 0.1 fusion.20
  54.3 0.1 fusion.21
  54.5 3.5 %collective-permute-start.3 = (f32[1,169]{1,0:T(1,128)S(1)}, f32[1,169]{1,0:T(1,128)S(1)}, u32[]{:S(2)}, u32[]{:S(2)}) collective-permute-start(f32[1,169]{1,0:T(1,128)S(1)} %bitcast.145), channel_id=1, source_target_pairs={{0,8},{8,16},{16,24},{1,9},{9,17},{17,25},{2,10},{10,18},{18,26},{... | collective-permute-start | bytes 2036 | tf_op jit(solution)/shard_map/ppermute | solution.py:21
  58.0 2.0 %collective-permute-done.3 = f32[1,169]{1,0:T(1,128)S(1)} collective-permute-done((f32[1,169]{1,0:T(1,128)S(1)}, f32[1,169]{1,0:T(1,128)S(1)}, u32[]{:S(2)}, u32[]{:S(2)}) %collective-permute-start.3) | collective-permute-done | bytes 708 | tf_op jit(solution)/shard_map/ppermute | solution.py:21
  59.9 1.9 %collective-permute-start.4 = (f32[2,1,169]{2,1,0:T(1,128)S(1)}, f32[2,1,169]{2,1,0:T(1,128)S(1)}, u32[]{:S(2)}, u32[]{:S(2)}) collective-permute-start(f32[2,1,169]{2,1,0:T(1,128)S(1)} %pad_maximum_fusion.2), channel_id=1, source_target_pairs={{0,2},{2,4},{4,6},{1,3},{3,5},{5,7},{8,10},{10,12},{12,14},{9,11},... | collective-permute-start | bytes 4064 | tf_op jit(solution)/shard_map/ppermute | solution.py:21
  61.9 3.0 %collective-permute-done.4 = f32[2,1,169]{2,1,0:T(1,128)S(1)} collective-permute-done((f32[2,1,169]{2,1,0:T(1,128)S(1)}, f32[2,1,169]{2,1,0:T(1,128)S(1)}, u32[]{:S(2)}, u32[]{:S(2)}) %collective-permute-start.4) | collective-permute-done | bytes 1384 | tf_op jit(solution)/shard_map/ppermute | solution.py:21
  64.8 1.3 %collective-permute-start.5 = (f32[2,2,1,169]{3,2,1,0:T(1,128)S(1)}, f32[2,2,1,169]{3,2,1,0:T(1,128)S(1)}, u32[]{:S(2)}, u32[]{:S(2)}) collective-permute-start(f32[2,2,1,169]{3,2,1,0:T(1,128)S(1)} %pad_maximum_fusion.1), channel_id=1, source_target_pairs={{0,1},{2,3},{4,5},{6,7},{8,9},{10,11},{12,13},{14,15},{16,17},{18,... | collective-permute-start | bytes 8120 | tf_op jit(solution)/shard_map/ppermute | solution.py:21
  66.1 4.2 %collective-permute-done.5 = f32[2,2,1,169]{3,2,1,0:T(1,128)S(1)} collective-permute-done((f32[2,2,1,169]{3,2,1,0:T(1,128)S(1)}, f32[2,2,1,169]{3,2,1,0:T(1,128)S(1)}, u32[]{:S(2)}, u32[]{:S(2)}) %collective-permute-start.5) | collective-permute-done | bytes 2736 | tf_op jit(solution)/shard_map/ppermute | solution.py:21
  70.4 0.1 dot_general.51
  70.4 0.2 fusion.16
  70.7 0.3 fusion
  71.0 0.7 copy.54
  (45 shorter events, 0.9 us)
Async XLA Ops:
  0.6 70.0 %copy-start = (f32[1,8,13,256]{3,1,2,0:T(8,128)S(1)}, f32[1,8,13,256]{3,1,2,0:T(8,128)}, u32[]{:S(2)}) copy-start(f32[1,8,13,256]{3,1,2,0:T(8,128)} %param.19) | copy-start | bytes 319492
  1.4 34.5 %copy-start.2 = (f32[4]{0:T(128)S(1)}, f32[4]{0:T(128)}, u32[]{:S(2)}) copy-start(f32[4]{0:T(128)} %param.14) | copy-start | bytes 52
  34.7 4.6 %copy-start.6 = (s32[1,8]{1,0:T(1,128)S(1)}, s32[1,8]{1,0:T(1,128)}, u32[]{:S(2)}) copy-start(s32[1,8]{1,0:T(1,128)} %param.16) | copy-start | bytes 100
  34.7 4.6 %copy-start.7 = (s32[32]{0:T(128)S(1)}, s32[32]{0:T(128)}, u32[]{:S(2)}) copy-start(s32[32]{0:T(128)} %param.15) | copy-start | bytes 388
  34.7 7.4 %copy-start.3 = (f32[4,9,169]{2,0,1:T(4,128)S(1)}, f32[4,9,169]{2,0,1:T(4,128)}, u32[]{:S(2)}) copy-start(f32[4,9,169]{2,0,1:T(4,128)} %param.12) | copy-start | bytes 73012
  34.7 7.4 %copy-start.1 = (f32[4,169,169]{2,0,1:T(4,128)S(1)}, f32[4,169,169]{2,0,1:T(4,128)}, u32[]{:S(2)}) copy-start(f32[4,169,169]{2,0,1:T(4,128)} %param.13) | copy-start | bytes 1370932
  35.6 7.1 %copy-start.4 = (f32[1,169]{1,0:T(1,128)S(1)}, f32[1,169]{1,0:T(1,128)}, u32[]{:S(2)}) copy-start(f32[1,169]{1,0:T(1,128)} %param.11) | copy-start | bytes 2032
  39.8 7.2 %collective-permute-start = (f32[2,2,1,9]{3,1,0,2:T(2,128)S(1)}, f32[2,2,1,9]{3,1,0,2:T(2,128)S(1)}, u32[]{:S(2)}, u32[]{:S(2)}) collective-permute-start(f32[2,2,1,9]{3,1,0,2:T(2,128)S(1)} %bitcast.163), channel_id=1, source_target_pairs={{8,0},{16,8},{24,16},{9,1},{17,9},{25,17},{10,2},{18,10},{26,18},{... | collective-permute-start | bytes 440 | tf_op jit(solution)/shard_map/ppermute | solution.py:21
  47.0 3.2 %collective-permute-start.1 = (f32[2,1,9]{2,0,1:T(2,128)S(1)}, f32[2,1,9]{2,0,1:T(2,128)S(1)}, u32[]{:S(2)}, u32[]{:S(2)}) collective-permute-start(f32[2,1,9]{2,0,1:T(2,128)S(1)} %slice_bitcast_fusion), channel_id=1, source_target_pairs={{2,0},{4,2},{6,4},{3,1},{5,3},{7,5},{10,8},{12,10},{14,12},{11,9},... | collective-permute-start | bytes 224 | tf_op jit(solution)/shard_map/ppermute | solution.py:21
  50.2 3.7 %collective-permute-start.2 = (f32[1,9]{1,0:T(1,128)S(1)}, f32[1,9]{1,0:T(1,128)S(1)}, u32[]{:S(2)}, u32[]{:S(2)}) collective-permute-start(f32[1,9]{1,0:T(1,128)S(1)} %slice_bitcast_fusion.2), channel_id=1, source_target_pairs={{1,0},{3,2},{5,4},{7,6},{9,8},{11,10},{13,12},{15,14},{17,16},{19,... | collective-permute-start | bytes 116 | tf_op jit(solution)/shard_map/ppermute | solution.py:21
  54.4 17.3 %copy-start.5 = (f32[169]{0:T(256)}, f32[169]{0:T(256)S(1)}, u32[]{:S(2)}) copy-start(f32[169]{0:T(256)S(1)} %multiply_add_fusion.1) | copy-start | bytes 2032
  54.5 5.5 %collective-permute-start.3 = (f32[1,169]{1,0:T(1,128)S(1)}, f32[1,169]{1,0:T(1,128)S(1)}, u32[]{:S(2)}, u32[]{:S(2)}) collective-permute-start(f32[1,169]{1,0:T(1,128)S(1)} %bitcast.145), channel_id=1, source_target_pairs={{0,8},{8,16},{16,24},{1,9},{9,17},{17,25},{2,10},{10,18},{18,26},{... | collective-permute-start | bytes 2036 | tf_op jit(solution)/shard_map/ppermute | solution.py:21
  59.9 4.9 %collective-permute-start.4 = (f32[2,1,169]{2,1,0:T(1,128)S(1)}, f32[2,1,169]{2,1,0:T(1,128)S(1)}, u32[]{:S(2)}, u32[]{:S(2)}) collective-permute-start(f32[2,1,169]{2,1,0:T(1,128)S(1)} %pad_maximum_fusion.2), channel_id=1, source_target_pairs={{0,2},{2,4},{4,6},{1,3},{3,5},{5,7},{8,10},{10,12},{12,14},{9,11},... | collective-permute-start | bytes 4064 | tf_op jit(solution)/shard_map/ppermute | solution.py:21
  64.8 5.5 %collective-permute-start.5 = (f32[2,2,1,169]{3,2,1,0:T(1,128)S(1)}, f32[2,2,1,169]{3,2,1,0:T(1,128)S(1)}, u32[]{:S(2)}, u32[]{:S(2)}) collective-permute-start(f32[2,2,1,169]{3,2,1,0:T(1,128)S(1)} %pad_maximum_fusion.1), channel_id=1, source_target_pairs={{0,1},{2,3},{4,5},{6,7},{8,9},{10,11},{12,13},{14,15},{16,17},{18,... | collective-permute-start | bytes 8120 | tf_op jit(solution)/shard_map/ppermute | solution.py:21
where the time goes:
time: 72.7 us; the launch traced here: 71.7 us
  local copies, waits for them, and re-layouts  36.7 us (50%)
  starting transfers between devices  13.4 us (18%)
  waiting for transfers between devices  11.7 us (16%)
  between operations  4.24 us (6%)
  matrix products  2.92 us (4%)
  other arithmetic  2.67 us (4%)
    gather x24, local copies, waits for them, and re-layouts  29.7 us
    ppermute x6, starting transfers between devices, shifted(): return lax.ppermute(x, axis, pairs)  13.4 us
    ppermute x6, waiting for transfers between devices, shifted(): return lax.ppermute(x, axis, pairs)  11.7 us
    pad x1, local copies, waits for them, and re-layouts, local(): jnp.pad(potential, ((margin, margin), (margin, margin), (margin, margin)))  3.41 us
  transfers between devices with their start and end apart: 6, of which 5 were waited for; matrix products, arithmetic and copies ran while one was open for 3% of the time, Pallas kernels for 0%

commit v1 on v0

v1 whole, which is shorter than its diff:
```python
import functools
import math

import jax
import jax.numpy as jnp
from jax import lax
from jax.experimental import pallas as pl
from jax.experimental.pallas import tpu as pltpu
from jax.sharding import PartitionSpec as P

BOX = 16
GROUP = 16
LANES = 128
AXES = ("gx", "gy", "gz")
HALF = (BOX - 1) / 2.0
harmonic_scale = 0.5 / math.sqrt(3.0)
f32 = jnp.float32
bf16 = jnp.bfloat16


def dot(a, b):
    return jnp.dot(a, b, preferred_element_type=f32)


def split(x):
    high = x.astype(bf16)
    return high, (x - high.astype(f32)).astype(bf16)


def lanes_of(shape):
    return lax.broadcasted_iota(jnp.int32, shape, len(shape) - 1)


def quotient(x, by):
    return jnp.floor((x + 0.5) * (1.0 / by))


def front(
    dims,
    cells_y,
    atom_ref,
    corner_ref,
    count_ref,
    species_ref,
    radius_ref,
    density_ref,
    delta_ref,
    potential_hbm,
    coulomb_hbm,
    pay_ref,
    dt_high_ref,
    dt_low_ref,
    spread_ref,
    pick_ref,
    v_ref,
    c_ref,
    dt_ref,
    sems,
):
    _, ny, nz = dims
    devices = pay_ref.shape[0]
    slots = atom_ref.shape[1]
    kinds, shapes, pairs = delta_ref.shape
    cells, size_z = v_ref.shape
    index_x, index_y, index_z = (lax.axis_index(a) for a in AXES)
    me = (index_x * ny + index_y) * nz + index_z
    v_copy = pltpu.make_async_copy(potential_hbm, v_ref, sems.at[0])
    v_copy.start()
    c_copy = pltpu.make_async_copy(coulomb_hbm.at[species_ref[me]], c_ref, sems.at[1])
    c_copy.start()

    tile = (8, LANES)
    row = lax.broadcasted_iota(jnp.int32, tile, 0)
    lane = lanes_of(tile)
    zero = jnp.zeros(tile, f32)
    kx, ky, kz, alive, radius = zero, zero, zero, zero, jnp.ones(tile, f32)
    group = lanes_of((GROUP, LANES)) // GROUP
    atom_lane = lanes_of((GROUP, devices))
    dt_ref[...] = jnp.zeros(dt_ref.shape, f32)
    for s in range(slots):
        live = s < count_ref[0]
        atom = atom_ref[0, s]
        kind = species_ref[atom]
        x, y, z = corner_ref[0, 0, s], corner_ref[1, 0, s], corner_ref[2, 0, s]
        code = (
            jnp.where(x < 0, 4, 0) + jnp.where(y < 0, 2, 0) + jnp.where(z < 0, 1, 0)
        )
        hit = row == jnp.where(live, code, 8)
        kx = jnp.where(hit, x.astype(f32), kx)
        ky = jnp.where(hit, y.astype(f32), ky)
        kz = jnp.where(hit, z.astype(f32), kz)
        radius = jnp.where(hit, radius_ref[kind], radius)
        alive = jnp.where(hit, 1.0, alive)
        rows = slice(s * GROUP, (s + 1) * GROUP)
        spread_ref[rows, :] = jnp.where(group == jnp.where(live, code, 8), 1.0, 0.0)
        pick_ref[rows, :] = jnp.where(atom_lane == jnp.where(live, atom, -1), 1.0, 0.0)

        @pl.when(live)
        def _():
            at = pl.ds(pl.multiple_of(code * GROUP, GROUP), shapes)
            dt_ref[at, :pairs] = delta_ref[kind]

    own = slice(slots * GROUP, slots * GROUP + 8)
    spread_ref[own, :] = jnp.where(group[:8] == 0, 1.0, 0.0)
    pick_ref[own, :] = jnp.where(atom_lane[:8] == me, 1.0, 0.0)
    dt_high_ref[...], dt_low_ref[...] = split(dt_ref[...])

    inverse = 1.0 / radius
    line = (lane.astype(f32) - HALF) * inverse
    line = jnp.where(lane < BOX, jnp.exp(-line * line), 0.0)
    line = jnp.sum(line, axis=1, keepdims=True)
    norm = alive / (line * line * line)

    def over(x, width):
        return jnp.concatenate([x] * (width // LANES), axis=1)

    def axis_of(position, corner, width):
        offset = position - over(corner, width)
        inside = (offset >= 0.0) & (offset < BOX)
        return (offset - HALF) * over(inverse, width), inside

    cell = lanes_of((8, cells)).astype(f32)
    cell_x = quotient(cell, cells_y)
    u, in_x = axis_of(cell_x, kx, cells)
    v, in_y = axis_of(cell - cell_x * cells_y, ky, cells)
    e = jnp.where(in_x & in_y, jnp.exp(-(u * u + v * v)), 0.0)
    eu, ev = e * u, e * v
    weights = jnp.concatenate([e, eu, ev, eu * v, eu * u, ev * v], axis=0)
    w_high, w_low = split(weights)
    w, in_z = axis_of(lanes_of((8, size_z)).astype(f32), kz, size_z)
    g = jnp.where(in_z, jnp.exp(-w * w), 0.0)
    gw = g * w

    c_copy.wait()
    density = jnp.broadcast_to(density_ref[...], (8, pairs))
    c_high, c_low = split(c_ref[...])
    d_high, d_low = split(density)
    contract = functools.partial(
        lax.dot_general,
        dimension_numbers=(((1,), (1,)), ((), ())),
        preferred_element_type=f32,
    )
    field = contract(d_high, c_high) + contract(d_high, c_low) + contract(d_low, c_high)
    field = 2.0 * field[:1]
    pay_ref[:, LANES + LANES :] = jnp.zeros((devices, LANES), f32)
    pay_ref[:, LANES : LANES + pairs] = jnp.broadcast_to(field, (devices, pairs))

    v_copy.wait()
    v_high, v_low = split(v_ref[...])
    both = dot(jnp.concatenate([w_high, w_low], axis=0), v_high)
    m = both[:48] + both[48:] + dot(w_high, v_low)
    m0, mu, mv, muv, muu, mvv = (m[8 * i : 8 * i + 8] for i in range(6))
    parts = [
        m0 * g,
        mu * g,
        mv * g,
        m0 * gw,
        muv * g,
        mv * gw,
        mu * gw,
        0.5 * (muu - mvv) * g,
        harmonic_scale * (2.0 * m0 * (gw * w) - (muu + mvv) * g),
    ]
    tiled = zero
    for i, part in enumerate(parts):
        total = jnp.sum(part, axis=1, keepdims=True)
        tiled = jnp.where(lane % GROUP == i, total, tiled)
    tiled = tiled * norm

    ky_step = 2 * nz + 2
    kx_step = ky_step * (2 * ny + 2)
    wide = (devices, LANES)
    e_index = lax.broadcasted_iota(jnp.int32, wide, 0).astype(f32)
    e_xy = quotient(e_index, nz)
    e_x = quotient(e_xy, ny)
    e_key = e_x * kx_step + (e_xy - e_x * ny) * ky_step + (e_index - e_xy * nz)
    my_key = index_x * kx_step + index_y * ky_step + index_z
    target = lanes_of(wide) // GROUP
    t_key = (target // 4) * kx_step + (target // 2 % 2) * ky_step + target % 2
    gap = t_key.astype(f32) - e_key + my_key.astype(f32)
    sent = jnp.zeros(wide, f32)
    for c in range(8):
        c_key = (c // 4) * kx_step + (c // 2 % 2) * ky_step + c % 2
        sent = jnp.where(gap == float(c_key), tiled[c : c + 1], sent)
    pay_ref[:, :LANES] = sent


def back(got_ref, dt_high_ref, dt_low_ref, spread_ref, pick_ref, projections_ref, dh_ref, applied_ref, p_ref):
    slots, projectors, bands = projections_ref.shape
    pairs = dh_ref.shape[1]
    rows = slots * GROUP
    got = got_ref[...]
    totals = jnp.sum(got[:, :LANES], axis=0, keepdims=True)
    s_high, s_low = split(spread_ref[...] * totals)
    m_high, m_low = split(got[:, LANES:])
    pick = pick_ref[...].astype(bf16)
    d_high = dt_high_ref[...]
    h = (
        dot(s_high, d_high)
        + dot(s_low, d_high)
        + dot(s_high, dt_low_ref[...])
        + dot(pick, m_high)
        + dot(pick, m_low)
    )
    dh_ref[...] = h[rows : rows + 1, :pairs]
    h = h[:rows]
    width = h.shape[1]
    p = lanes_of((rows, width)).astype(f32)
    j = p - quotient(p, projectors) * projectors
    slot_row = lax.broadcasted_iota(jnp.int32, (rows, width), 0)
    keep = (j == (slot_row % GROUP).astype(f32)) & (p < pairs)
    h_high, h_low = split(jnp.where(keep, h, 0.0))
    q_row = quotient(lax.broadcasted_iota(jnp.int32, (width, rows), 0).astype(f32), projectors)
    move = jnp.where(q_row == (lanes_of((width, rows)) % GROUP).astype(f32), 1.0, 0.0).astype(bf16)
    block = dot(jnp.concatenate([h_high, h_low], axis=0), move)
    b_row = lax.broadcasted_iota(jnp.int32, (2 * rows, rows), 0) % rows
    diagonal = b_row // GROUP == lanes_of((2 * rows, rows)) // GROUP
    block = jnp.where(diagonal, block, 0.0).astype(bf16)
    p_ref[...] = jnp.zeros(p_ref.shape, f32)
    for s in range(slots):
        p_ref[s * GROUP : s * GROUP + projectors, :] = projections_ref[s]
    p_high, p_low = split(p_ref[...])
    both = dot(block, p_high)
    out = both[:rows] + both[rows:] + dot(block[:rows], p_low)
    for s in range(slots):
        applied_ref[s] = out[s * GROUP : s * GROUP + projectors]


def local(
    potential,
    density_matrix,
    delta_table,
    coulomb,
    radius,
    atom_species,
    slot_atom,
    slot_corner,
    slot_count,
    projections,
):
    dims = tuple(lax.axis_size(a) for a in AXES)
    devices = math.prod(dims)
    assert density_matrix.shape[0] == 1 and slot_atom.shape[1] == 8
    slots = slot_atom.shape[1]
    size_x, size_y, size_z = potential.shape
    pairs = density_matrix.shape[1]
    columns = 2 * LANES
    rows = slots * GROUP
    smem = pl.BlockSpec(memory_space=pltpu.SMEM)
    vmem = pl.BlockSpec(memory_space=pltpu.VMEM)
    hbm = pl.BlockSpec(memory_space=pl.ANY)
    pay, dt_high, dt_low, spread, pick = pl.pallas_call(
        functools.partial(front, dims, size_y),
        out_shape=(
            jax.ShapeDtypeStruct((devices, LANES + columns), f32),
            jax.ShapeDtypeStruct((8 * GROUP, columns), bf16),
            jax.ShapeDtypeStruct((8 * GROUP, columns), bf16),
            jax.ShapeDtypeStruct((rows + 8, LANES), f32),
            jax.ShapeDtypeStruct((rows + 8, devices), f32),
        ),
        in_specs=[smem] * 5 + [vmem] * 2 + [hbm] * 2,
        out_specs=[vmem] * 5,
        scratch_shapes=[
            pltpu.VMEM((size_x * size_y, size_z), f32),
            pltpu.VMEM((pairs, pairs), f32),
            pltpu.VMEM((8 * GROUP, columns), f32),
            pltpu.SemaphoreType.DMA((2,)),
        ],
    )(
        slot_atom,
        slot_corner,
        slot_count,
        atom_species,
        radius,
        density_matrix,
        delta_table,
        potential.reshape(size_x * size_y, size_z),
        coulomb,
    )
    got = lax.all_to_all(pay, AXES, 0, 0, tiled=True)
    dh, applied = pl.pallas_call(
        back,
        out_shape=(
            jax.ShapeDtypeStruct(density_matrix.shape, f32),
            jax.ShapeDtypeStruct(projections.shape[1:], f32),
        ),
        in_specs=[vmem] * 6,
        out_specs=[vmem] * 2,
        scratch_shapes=[pltpu.VMEM((rows, projections.shape[3]), f32)],
    )(got, dt_high, dt_low, spread, pick, projections[0])
    return dh, applied[None]


def solution(mesh):
    return jax.shard_map(
        local,
        mesh=mesh,
        in_specs=(
            P("gx", "gy", "gz"),
            P(AXES, None),
            P(),
            P(),
            P(),
            P(),
            P(AXES, None),
            P(None, AXES, None),
            P(AXES),
            P(AXES, None, None, None),
        ),
        out_specs=(P(AXES, None), P(AXES, None, None, None)),
        check_vma=False,
    )
```

time: 72.7 us -> 28.4 us (0.39)
  the two profiles are of different devices: /device:TPU:14 before, /device:TPU:0 now
where the time goes in v1:
time: 28.4 us; the launch traced here: 28.1 us
  starting transfers between devices  7.32 us (26%)
  local copies, waits for them, and re-layouts  7.14 us (25%)
  waiting for transfers between devices  6.79 us (24%)
  Pallas kernels  5.5 us (19%)
  between operations  1.32 us (5%)
    all_to_all x1, starting transfers between devices, local(): got = lax.all_to_all(pay, AXES, 0, 0, tiled=True)  7.32 us
    all_to_all x1, waiting for transfers between devices, local(): got = lax.all_to_all(pay, AXES, 0, 0, tiled=True)  6.79 us
    unnamed x9, local copies, waits for them, and re-layouts  5.65 us
    pallas_call x1, Pallas kernels, local(): pl.pallas_call(functools.partial(front, dims, size_y), out_shape=(jax.Sha...  3.17 us
    pallas_call x1, Pallas kernels, local(): pl.pallas_call(back, out_shape=(jax.ShapeDtypeStruct(density_matrix.shape...  2.33 us
    all_to_all x1, local copies, waits for them, and re-layouts, local(): got = lax.all_to_all(pay, AXES, 0, 0, tiled=True)  1.49 us
  transfers between devices with their start and end apart: 1, of which 1 were waited for; matrix products, arithmetic and copies ran while one was open for 2% of the time, Pallas kernels for 0%

profile of v1, /device:TPU:0, one launch (start us, length us, event | category | flops | bytes accessed | tf_op | source)
XLA Modules:
  0.0 28.1 jit_solution(9957916699042268478)
XLA Ops:
  0.6 0.0 copy-start.1
  0.6 2.1 %copy.17.coulomb_hbm = f32[4,169,169]{2,1,0:T(8,128)} copy(f32[4,169,169]{2,0,1:T(4,128)} %param.13) | data formatting | bytes 913952 | tf_op args[3]
  2.7 0.0 copy-done.1
  2.7 0.6 %copy.16.delta_ref = f32[4,9,169]{2,1,0:T(8,128)} copy(f32[4,9,169]{2,0,1:T(4,128)S(1)} %copy-done.1) | data formatting | bytes 48672 | tf_op args[2]
  4.0 3.2 %shard_map.113 = (f32[32,384]{1,0:T(8,128)}, bf16[128,256]{1,0:T(8,128)(2,1)}, bf16[128,256]{1,0:T(8,128)(2,1)}, f32[136,128]{1,0:T(8,128)}, f32[136,32]{1,0:T(8,128)}) custom-call(s32[1,8]{1,0:T(1,128)} %atom_ref.1, s32[3,1,8]{2,1,0:T(1,128)} %corner_ref.1, s32[1]{0:T(128)S(6)} %copy.26.count_ref, s32[32]{0:T(128)} %species_ref.1, f32[4]{0:T(128)} %radius_ref.1, ...), custom_call_target="tpu_custom_call" | custom-call | tf_op jit(solution)/shard_map/pallas_call | solution.py:252
  7.2 0.0 copy-start
  7.2 1.5 %copy.18 = f32[32,1,384]{2,1,0:T(1,128)} copy(f32[32,1,384]{2,0,1:T(8,128)} %bitcast.13) | data formatting | bytes 98304 | tf_op jit(solution)/shard_map/all_to_all | solution.py:280
  8.7 7.3 %all-to-all-start = ((f32[32,1,384]{2,1,0:T(1,128)}), f32[32,1,384]{2,1,0:T(1,128)S(1)}, u32[]{:S(2)}, u32[]{:S(2)}) async-start(f32[32,1,384]{2,1,0:T(1,128)} %copy.18), calls=%async_computation | async-start | bytes 98304 | tf_op jit(solution)/shard_map/all_to_all | solution.py:280
  16.0 0.0 copy-done
  16.0 0.7 %copy.24 = f32[1,8,13,256]{3,2,1,0:T(8,128)} copy(f32[1,8,13,256]{3,1,2,0:T(8,128)S(1)} %copy-done) | data formatting | bytes 212992 | tf_op args[9]
  16.7 6.8 %all-to-all-done = f32[32,1,384]{2,1,0:T(1,128)S(1)} async-done(((f32[32,1,384]{2,1,0:T(1,128)}), f32[32,1,384]{2,1,0:T(1,128)S(1)}, u32[]{:S(2)}, u32[]{:S(2)}) %all-to-all-start) | async-done | bytes 49184 | tf_op jit(solution)/shard_map/all_to_all | solution.py:280
  23.5 0.6 %copy.25 = f32[32,1,384]{2,0,1:T(8,128)} copy(f32[32,1,384]{2,1,0:T(1,128)S(1)} %all-to-all-done) | data formatting | bytes 98304
  24.1 2.3 %shard_map.114 = (f32[1,169]{1,0:T(1,128)}, f32[8,13,256]{2,1,0:T(8,128)}) custom-call(f32[32,384]{1,0:T(8,128)} %bitcast.11, bf16[128,256]{1,0:T(8,128)(2,1)} %get-tuple-element.10.dt_high_ref, bf16[128,256]{1,0:T(8,128)(2,1)} %get-tuple-element.11.dt_low_ref, f32[136,128]{1,0:T(8,128)} %get-tuple-element.12.spread_ref, ...), custom_call_target="tpu_custom_call" | custom-call | tf_op jit(solution)/shard_map/pallas_call | solution.py:281
  26.5 1.6 %copy.20 = f32[1,8,13,256]{3,1,2,0:T(8,128)} copy(f32[1,8,13,256]{3,2,1,0:T(8,128)} %bitcast.12) | data formatting | bytes 212992
Async XLA Ops:
  0.6 2.1 %copy-start.1 = (f32[4,9,169]{2,0,1:T(4,128)S(1)}, f32[4,9,169]{2,0,1:T(4,128)}, u32[]{:S(2)}) copy-start(f32[4,9,169]{2,0,1:T(4,128)} %param.12) | copy-start | bytes 73012
  7.2 8.8 %copy-start = (f32[1,8,13,256]{3,1,2,0:T(8,128)S(1)}, f32[1,8,13,256]{3,1,2,0:T(8,128)}, u32[]{:S(2)}) copy-start(f32[1,8,13,256]{3,1,2,0:T(8,128)} %param.19) | copy-start | bytes 319492
  8.7 14.8 %all-to-all-start = ((f32[32,1,384]{2,1,0:T(1,128)}), f32[32,1,384]{2,1,0:T(1,128)S(1)}, u32[]{:S(2)}, u32[]{:S(2)}) async-start(f32[32,1,384]{2,1,0:T(1,128)} %copy.18), calls=%async_computation | async-start | bytes 98304 | tf_op jit(solution)/shard_map/all_to_all | solution.py:280

commit v2 on v1

v2 whole, which is shorter than its diff:
```python
import functools
import math

import jax
import jax.numpy as jnp
from jax import lax
from jax.experimental import pallas as pl
from jax.experimental.pallas import tpu as pltpu
from jax.sharding import PartitionSpec as P

BOX = 16
CODES = 8
LANES = 128
AXES = ("gx", "gy", "gz")
HALF = (BOX - 1) / 2.0
VMEM_BYTES = 8 << 20
harmonic_scale = 0.5 / math.sqrt(3.0)
f32 = jnp.float32
bf16 = jnp.bfloat16
TILE = (CODES, LANES)


def dot(a, b):
    return jnp.dot(a, b, preferred_element_type=f32)


def split(x):
    high = x.astype(bf16)
    return high, (x - high.astype(f32)).astype(bf16)


def lanes_of(shape):
    return lax.broadcasted_iota(jnp.int32, shape, len(shape) - 1)


def quotient(x, by):
    return jnp.floor((x + 0.5) * (1.0 / by))


def front(
    dims,
    cells_y,
    atom_hbm,
    corner_hbm,
    species_hbm,
    radius_hbm,
    density_hbm,
    potential_hbm,
    coulomb_hbm,
    pay_ref,
    kinds_ref,
    codes_ref,
    atom_ref,
    corner_ref,
    species_ref,
    radius_ref,
    density_ref,
    v_ref,
    c_ref,
    sems,
):
    _, ny, nz = dims
    slots = atom_ref.shape[1]
    cells, size_z = v_ref.shape
    pairs, kinds, _ = c_ref.shape
    sources = (atom_hbm, corner_hbm, species_hbm, radius_hbm, density_hbm, potential_hbm, coulomb_hbm)
    targets = (atom_ref, corner_ref, species_ref, radius_ref, density_ref, v_ref, c_ref)
    copies = [pltpu.make_async_copy(s, t, sems.at[i]) for i, (s, t) in enumerate(zip(sources, targets))]
    for copy in copies:
        copy.start()
    index_x, index_y, index_z = (lax.axis_index(a) for a in AXES)
    me = (index_x * ny + index_y) * nz + index_z
    row = lax.broadcasted_iota(jnp.int32, TILE, 0)
    lane = lanes_of(TILE)
    zero = jnp.zeros(TILE, f32)
    for copy in copies[:4]:
        copy.wait()

    kx, ky, kz, alive, radius, kind_of = zero, zero, zero, zero, jnp.ones(TILE, f32), zero
    codes = jnp.full(TILE, -1.0, f32)
    for s in range(slots):
        atom = atom_ref[0, s]
        kind = species_ref[atom]
        x, y, z = corner_ref[0, 0, s], corner_ref[1, 0, s], corner_ref[2, 0, s]
        code = jnp.where(x < 0, 4, 0) + jnp.where(y < 0, 2, 0) + jnp.where(z < 0, 1, 0)
        if s > 0:
            code = jnp.where((atom == 0) & (x == 0) & (y == 0) & (z == 0), -1, code)
        hit = row == code
        kx = jnp.where(hit, x.astype(f32), kx)
        ky = jnp.where(hit, y.astype(f32), ky)
        kz = jnp.where(hit, z.astype(f32), kz)
        radius = jnp.where(hit, radius_ref[kind], radius)
        kind_of = jnp.where(hit, kind.astype(f32), kind_of)
        alive = jnp.where(hit, 1.0, alive)
        codes = jnp.where(row == s, code.astype(f32), codes)
    kinds_ref[...] = kind_of
    codes_ref[...] = codes

    inverse = 1.0 / radius
    line = (lane.astype(f32) - HALF) * inverse
    line = jnp.where(lane < BOX, jnp.exp(-line * line), 0.0)
    line = jnp.sum(line, axis=1, keepdims=True)
    norm = alive / (line * line * line)

    def over(x, width):
        return jnp.concatenate([x] * (width // LANES), axis=1)

    def axis_of(position, corner, width):
        offset = position - over(corner, width)
        inside = (offset >= 0.0) & (offset < BOX)
        return (offset - HALF) * over(inverse, width), inside

    cell = lanes_of((CODES, cells)).astype(f32)
    cell_x = quotient(cell, cells_y)
    u, in_x = axis_of(cell_x, kx, cells)
    v, in_y = axis_of(cell - cell_x * cells_y, ky, cells)
    e = jnp.where(in_x & in_y, jnp.exp(-(u * u + v * v)), 0.0)
    eu, ev = e * u, e * v
    weights = jnp.concatenate([e, eu, ev, eu * v, eu * u, ev * v], axis=0)
    w_high, w_low = split(weights)
    w, in_z = axis_of(lanes_of((CODES, size_z)).astype(f32), kz, size_z)
    g = jnp.where(in_z, jnp.exp(-w * w), 0.0)
    gw = g * w

    copies[5].wait()
    v_high, v_low = split(v_ref[...])
    both = dot(jnp.concatenate([w_high, w_low], axis=0), v_high)
    m = both[: 6 * CODES] + both[6 * CODES :] + dot(w_high, v_low)
    m0, mu, mv, muv, muu, mvv = (m[CODES * i : CODES * (i + 1)] for i in range(6))
    parts = [
        m0 * g,
        mu * g,
        mv * g,
        m0 * gw,
        muv * g,
        mv * gw,
        mu * gw,
        0.5 * (muu - mvv) * g,
        harmonic_scale * (2.0 * m0 * (gw * w) - (muu + mvv) * g),
    ]
    partial = zero
    for i, part in enumerate(parts):
        partial = jnp.where(lane == i, jnp.sum(part, axis=1, keepdims=True), partial)
    pay_ref[:CODES] = partial * norm

    copies[4].wait()
    copies[6].wait()
    density = 2.0 * density_ref[...]
    small = lanes_of((kinds, LANES))
    lines = [jnp.zeros((kinds, LANES), f32) for _ in range(2)]
    for n in range(pairs):
        total = jnp.sum(c_ref[n] * density, axis=1, keepdims=True)
        lines[n // LANES] = jnp.where(small == n % LANES, total, lines[n // LANES])
    own = lax.broadcasted_iota(jnp.int32, (kinds, LANES), 0) == species_ref[me]
    for i, line in enumerate(lines):
        field = jnp.sum(jnp.where(own, line, 0.0), axis=0, keepdims=True)
        pay_ref[CODES * (i + 1) : CODES * (i + 2)] = jnp.where(row == 0, field, 0.0)


def prepare(kinds_ref, delta_ref, out_ref):
    shapes, kinds, pairs = delta_ref.shape
    out_ref[:, LANES:] = jnp.zeros((shapes * CODES, LANES), f32)
    kind = jnp.concatenate([kinds_ref[...]] * 2, axis=1)[:, :pairs]
    for i in range(shapes):
        rows = delta_ref[i]
        chosen = jnp.zeros((CODES, pairs), f32)
        for k in range(kinds):
            chosen = jnp.where(kind == float(k), rows[k : k + 1], chosen)
        out_ref[i * CODES : (i + 1) * CODES, :pairs] = chosen


def back(pay_ref, delta_ref, codes_ref, projections_ref, dh_ref, applied_ref):
    projectors = projections_ref.shape[0]
    bands = projections_ref.shape[2]
    pairs = dh_ref.shape[1]
    width = 2 * LANES
    totals = pay_ref[:CODES]
    h = jnp.concatenate([pay_ref[CODES : 2 * CODES], pay_ref[2 * CODES :]], axis=1)
    for i in range(delta_ref.shape[0] // CODES):
        h = h + jnp.broadcast_to(totals[:, i : i + 1], (CODES, width)) * delta_ref[i * CODES : (i + 1) * CODES]
    dh_ref[...] = h[:1, :pairs]
    codes = jnp.concatenate([codes_ref[...]] * 2, axis=1)
    by_slot = jnp.zeros((CODES, width), f32)
    for c in range(CODES):
        by_slot = jnp.where(codes == float(c), h[c : c + 1], by_slot)
    for j in range(projectors):
        out = jnp.zeros((CODES, bands), f32)
        for i in range(projectors):
            at = i * projectors + j
            out = out + jnp.broadcast_to(by_slot[:, at : at + 1], (CODES, bands)) * projections_ref[i]
        applied_ref[j] = out


def swaps(dims, axis, odd):
    nx, ny, nz = dims
    size = dims[axis]

    def partner(at):
        i = at[axis]
        other = i ^ 1 if not odd else (i + 1 ^ 1) - 1
        if 0 <= other < size:
            return at[:axis] + (other,) + at[axis + 1 :]
        if axis == 0 and at[1] ^ 1 < ny:
            return (at[0], at[1] ^ 1, at[2])
        if axis == 1 and odd and size % 2 == 0:
            return (at[0], size - 1 - i, at[2])
        return at

    def line(at):
        return (at[0] * ny + at[1]) * nz + at[2]

    every = [(x, y, z) for x in range(nx) for y in range(ny) for z in range(nz)]
    return [(line(at), line(partner(at))) for at in every]


def exchange(x, dims, axis):
    index = lax.axis_index(AXES[axis])
    even = index % 2 == 0
    first = lax.ppermute(x, AXES, swaps(dims, axis, False))
    second = lax.ppermute(x, AXES, swaps(dims, axis, True)) if dims[axis] > 2 else first
    up = jnp.where(even, first, second)
    down = jnp.where(even, second, first)
    step = CODES // 2 >> axis
    up = jnp.roll(up, -step, axis=0)
    down = jnp.roll(down, step, axis=0)
    row = lax.broadcasted_iota(jnp.int32, x.shape, 0)
    higher = row // step % 2 == 1
    partial = row < CODES
    has_up = index < dims[axis] - 1
    kept = jnp.where(partial & ~higher & has_up, x + up, x)
    return jnp.where(higher, jnp.where(partial, x + down, down), kept)


def local(
    potential,
    density_matrix,
    delta_table,
    coulomb,
    radius,
    atom_species,
    slot_atom,
    slot_corner,
    slot_count,
    projections,
):
    dims = tuple(lax.axis_size(a) for a in AXES)
    slots = slot_atom.shape[1]
    assert density_matrix.shape[0] == 1 and slots == CODES
    size_x, size_y, size_z = potential.shape
    pairs = density_matrix.shape[1]
    kinds, shapes, _ = delta_table.shape
    smem, vmem, hbm = (pl.BlockSpec(memory_space=m) for m in (pltpu.SMEM, pltpu.VMEM, pltpu.HBM))
    params = pltpu.CompilerParams(vmem_limit_bytes=VMEM_BYTES)
    tile = jax.ShapeDtypeStruct(TILE, f32)
    pay, kind_of, codes = pl.pallas_call(
        functools.partial(front, dims, size_y),
        out_shape=(pltpu.VMEM((3 * CODES, LANES), f32), pltpu.VMEM(TILE,f32), pltpu.VMEM(TILE,f32)),
        in_specs=[hbm] * 7,
        out_specs=[vmem] * 3,
        scratch_shapes=[
            pltpu.SMEM(slot_atom.shape, jnp.int32),
            pltpu.SMEM(slot_corner.shape, jnp.int32),
            pltpu.SMEM(atom_species.shape, jnp.int32),
            pltpu.SMEM(radius.shape, f32),
            pltpu.VMEM((1, pairs), f32),
            pltpu.VMEM((size_x * size_y, size_z), f32),
            pltpu.VMEM((pairs, kinds, pairs), f32),
            pltpu.SemaphoreType.DMA((7,)),
        ],
        compiler_params=params,
    )(*(pltpu.with_memory_space_constraint(x, pltpu.HBM) for x in (
        slot_atom,
        slot_corner,
        atom_species,
        radius,
        density_matrix,
        potential.reshape(size_x * size_y, size_z),
        coulomb.transpose(1, 0, 2),
    )))
    delta = pl.pallas_call(
        prepare,
        out_shape=jax.ShapeDtypeStruct((shapes * CODES, 2 * LANES), f32),
        in_specs=[vmem] * 2,
        out_specs=vmem,
        compiler_params=params,
        cost_estimate=pl.CostEstimate(flops=200000, bytes_accessed=200000, transcendentals=0),
    )(kind_of, delta_table.transpose(1, 0, 2))
    for axis in (2, 1, 0):
        pay = exchange(pay, dims, axis)
    bands = projections[0].transpose(1, 0, 2)
    dh, applied = pl.pallas_call(
        back,
        out_shape=(jax.ShapeDtypeStruct(density_matrix.shape, f32), jax.ShapeDtypeStruct(bands.shape, f32)),
        in_specs=[vmem] * 4,
        out_specs=[vmem] * 2,
        compiler_params=params,
    )(pay, delta, codes, bands)
    return dh, applied.transpose(1, 0, 2)[None]


def solution(mesh):
    return jax.shard_map(
        local,
        mesh=mesh,
        in_specs=(
            P("gx", "gy", "gz"),
            P(AXES, None),
            P(),
            P(),
            P(),
            P(),
            P(AXES, None),
            P(None, AXES, None),
            P(AXES),
            P(AXES, None, None, None),
        ),
        out_specs=(P(AXES, None), P(AXES, None, None, None)),
        check_vma=False,
    )
```

time: 28.4 us -> 16.2 us (0.57)
  the two profiles are of different devices: /device:TPU:0 before, /device:TPU:16 now
where the time goes in v2:
time: 16.2 us; the launch traced here: 16.1 us
  waiting for transfers between devices  7.36 us (45%)
  starting transfers between devices  4.84 us (30%)
  Pallas kernels  2.77 us (17%)
  between operations  0.75 us (5%)
  other arithmetic  0.31 us (2%)
    ppermute x3, waiting for transfers between devices, exchange(): first = lax.ppermute(x, AXES, swaps(dims, axis, False))  4.23 us
    ppermute x3, starting transfers between devices, exchange(): first = lax.ppermute(x, AXES, swaps(dims, axis, False))  3.21 us
    ppermute x2, waiting for transfers between devices, exchange(): lax.ppermute(x, AXES, swaps(dims, axis, True))  3.13 us
    pallas_call x1, Pallas kernels, local(): pl.pallas_call(functools.partial(front, dims, size_y), out_shape=(pltpu.V...  1.65 us
    ppermute x2, starting transfers between devices, exchange(): lax.ppermute(x, AXES, swaps(dims, axis, True))  1.62 us
    pallas_call x1, Pallas kernels, local(): pl.pallas_call(back, out_shape=(jax.ShapeDtypeStruct(density_matrix.shape...  1.1 us
  transfers between devices with their start and end apart: 5, of which 4 were waited for; matrix products, arithmetic and copies ran while one was open for 0% of the time, Pallas kernels for 0%

profile of v2, /device:TPU:16, one launch (start us, length us, event | category | flops | bytes accessed | tf_op | source)
XLA Modules:
  0.0 16.1 jit_solution(3718658834895507152)
XLA Ops:
  0.6 1.6 %shard_map.104 = (f32[24,128]{1,0:T(8,128)S(1)}, f32[8,128]{1,0:T(8,128)S(1)}, f32[8,128]{1,0:T(8,128)S(1)}) custom-call(s32[1,8]{1,0:T(1,128)} %atom_hbm.1, s32[3,1,8]{2,1,0:T(1,128)} %corner_hbm.1, s32[32]{0:T(128)} %species_hbm.1, f32[4]{0:T(128)} %radius_hbm.1, f32[1,169]{1,0:T(1,128)} %density_hbm.1, f32[768,128]{1,0:T(8,128)} %bitcast.14, ...), custom_call_target="tpu_custom_call" | custom-call | tf_op jit(solution)/shard_map/pallas_call | solution.py:255
  2.3 1.6 %collective-permute-start = (f32[24,128]{1,0:T(8,128)S(1)}, f32[24,128]{1,0:T(8,128)S(1)}, u32[]{:S(2)}, u32[]{:S(2)}) collective-permute-start(f32[24,128]{1,0:T(8,128)S(1)} %get-tuple-element.7), channel_id=1, source_target_pairs={{0,1},{1,0},{2,3},{3,2},{4,5},{5,4},{6,7},{7,6},{8,9},{9,8},{10,11... | collective-permute-start | bytes 36872 | tf_op jit(solution)/shard_map/ppermute | solution.py:219
  3.9 2.2 %collective-permute-done = f32[24,128]{1,0:T(8,128)S(1)} collective-permute-done((f32[24,128]{1,0:T(8,128)S(1)}, f32[24,128]{1,0:T(8,128)S(1)}, u32[]{:S(2)}, u32[]{:S(2)}) %collective-permute-start) | collective-permute-done | bytes 12320 | tf_op jit(solution)/shard_map/ppermute | solution.py:219
  6.1 0.1 fusion.3
  6.1 0.0 collective-permute-start.2
  6.2 1.6 %collective-permute-start.1 = (f32[24,128]{1,0:T(8,128)S(1)}, f32[24,128]{1,0:T(8,128)S(1)}, u32[]{:S(2)}, u32[]{:S(2)}) collective-permute-start(f32[24,128]{1,0:T(8,128)S(1)} %fusion.3), channel_id=1, source_target_pairs={{0,6},{1,7},{2,4},{3,5},{4,2},{5,3},{6,0},{7,1},{8,14},{9,15},{10,... | collective-permute-start | bytes 36872 | tf_op jit(solution)/shard_map/ppermute | solution.py:220
  7.8 0.0 collective-permute-done.2
  7.8 1.6 %collective-permute-done.1 = f32[24,128]{1,0:T(8,128)S(1)} collective-permute-done((f32[24,128]{1,0:T(8,128)S(1)}, f32[24,128]{1,0:T(8,128)S(1)}, u32[]{:S(2)}, u32[]{:S(2)}) %collective-permute-start.1) | collective-permute-done | bytes 12320 | tf_op jit(solution)/shard_map/ppermute | solution.py:220
  9.4 0.0 copy-start.1
  9.4 0.1 fusion.4
  9.5 1.6 %collective-permute-start.4 = (f32[24,128]{1,0:T(8,128)S(1)}, f32[24,128]{1,0:T(8,128)S(1)}, u32[]{:S(2)}, u32[]{:S(2)}) collective-permute-start(f32[24,128]{1,0:T(8,128)S(1)} %fusion.4), channel_id=1, source_target_pairs={{0,8},{1,9},{2,10},{3,11},{4,12},{5,13},{6,14},{7,15},{8,0},{9,1},... | collective-permute-start | bytes 36872 | tf_op jit(solution)/shard_map/ppermute | solution.py:219
  11.1 0.0 collective-permute-start.3
  11.1 0.0 copy-done.1
  11.2 0.0 copy-start
  11.2 2.0 %collective-permute-done.4 = f32[24,128]{1,0:T(8,128)S(1)} collective-permute-done((f32[24,128]{1,0:T(8,128)S(1)}, f32[24,128]{1,0:T(8,128)S(1)}, u32[]{:S(2)}, u32[]{:S(2)}) %collective-permute-start.4) | collective-permute-done | bytes 12320 | tf_op jit(solution)/shard_map/ppermute | solution.py:219
  13.3 1.6 %collective-permute-done.3 = f32[24,128]{1,0:T(8,128)S(1)} collective-permute-done((f32[24,128]{1,0:T(8,128)S(1)}, f32[24,128]{1,0:T(8,128)S(1)}, u32[]{:S(2)}, u32[]{:S(2)}) %collective-permute-start.3) | collective-permute-done | bytes 12320 | tf_op jit(solution)/shard_map/ppermute | solution.py:220
  14.9 0.1 fusion.5.pay_ref
  15.0 0.0 copy-done
  15.0 1.1 %shard_map.106 = (f32[1,169]{1,0:T(1,128)}, f32[13,8,256]{2,1,0:T(8,128)}) custom-call(f32[24,128]{1,0:T(8,128)S(1)} %fusion.5.pay_ref, f32[72,256]{1,0:T(8,128)S(1)} %shard_map.105.delta_ref, f32[8,128]{1,0:T(8,128)S(1)} %get-tuple-element.9.codes_ref, f32[13,8,256]{2,1,0:T(8,128)S(1)} %bitcast.11), custom_call_target="tpu_custom_call" | custom-call | tf_op jit(solution)/shard_map/pallas_call | solution.py:291
  (16 shorter events, 0.1 us)
Async XLA Ops:
  2.3 3.8 %collective-permute-start = (f32[24,128]{1,0:T(8,128)S(1)}, f32[24,128]{1,0:T(8,128)S(1)}, u32[]{:S(2)}, u32[]{:S(2)}) collective-permute-start(f32[24,128]{1,0:T(8,128)S(1)} %get-tuple-element.7), channel_id=1, source_target_pairs={{0,1},{1,0},{2,3},{3,2},{4,5},{5,4},{6,7},{7,6},{8,9},{9,8},{10,11... | collective-permute-start | bytes 36872 | tf_op jit(solution)/shard_map/ppermute | solution.py:219
  6.1 1.7 %collective-permute-start.2 = (f32[24,128]{1,0:T(8,128)S(1)}, f32[24,128]{1,0:T(8,128)S(1)}, u32[]{:S(2)}, u32[]{:S(2)}) collective-permute-start(f32[24,128]{1,0:T(8,128)S(1)} %fusion.3), channel_id=1, source_target_pairs={{0,2},{1,3},{2,0},{3,1},{4,6},{5,7},{6,4},{7,5},{8,10},{9,11},{10,... | collective-permute-start | bytes 36872 | tf_op jit(solution)/shard_map/ppermute | solution.py:219
  6.2 3.2 %collective-permute-start.1 = (f32[24,128]{1,0:T(8,128)S(1)}, f32[24,128]{1,0:T(8,128)S(1)}, u32[]{:S(2)}, u32[]{:S(2)}) collective-permute-start(f32[24,128]{1,0:T(8,128)S(1)} %fusion.3), channel_id=1, source_target_pairs={{0,6},{1,7},{2,4},{3,5},{4,2},{5,3},{6,0},{7,1},{8,14},{9,15},{10,... | collective-permute-start | bytes 36872 | tf_op jit(solution)/shard_map/ppermute | solution.py:220
  9.4 1.8 %copy-start.1 = (f32[4,9,169]{2,0,1:T(4,128)S(1)}, f32[4,9,169]{2,0,1:T(4,128)}, u32[]{:S(2)}) copy-start(f32[4,9,169]{2,0,1:T(4,128)} %param.12) | copy-start | bytes 73012
  9.5 3.8 %collective-permute-start.4 = (f32[24,128]{1,0:T(8,128)S(1)}, f32[24,128]{1,0:T(8,128)S(1)}, u32[]{:S(2)}, u32[]{:S(2)}) collective-permute-start(f32[24,128]{1,0:T(8,128)S(1)} %fusion.4), channel_id=1, source_target_pairs={{0,8},{1,9},{2,10},{3,11},{4,12},{5,13},{6,14},{7,15},{8,0},{9,1},... | collective-permute-start | bytes 36872 | tf_op jit(solution)/shard_map/ppermute | solution.py:219
  11.1 3.7 %collective-permute-start.3 = (f32[24,128]{1,0:T(8,128)S(1)}, f32[24,128]{1,0:T(8,128)S(1)}, u32[]{:S(2)}, u32[]{:S(2)}) collective-permute-start(f32[24,128]{1,0:T(8,128)S(1)} %fusion.4), channel_id=1, source_target_pairs={{0,2},{1,3},{2,0},{3,1},{4,6},{5,7},{6,4},{7,5},{8,16},{9,17},{10,... | collective-permute-start | bytes 36872 | tf_op jit(solution)/shard_map/ppermute | solution.py:220
  11.2 3.8 %copy-start = (f32[1,8,13,256]{3,1,2,0:T(8,128)S(1)}, f32[1,8,13,256]{3,1,2,0:T(8,128)}, u32[]{:S(2)}) copy-start(f32[1,8,13,256]{3,1,2,0:T(8,128)} %param.18) | copy-start | bytes 319492

commit v3 on v2

v3 whole, which is shorter than its diff:
```python
import functools
import math

import jax
import jax.numpy as jnp
from jax import lax
from jax.experimental import pallas as pl
from jax.experimental.pallas import tpu as pltpu
from jax.sharding import PartitionSpec as P

BOX = 16
CODES = 8
LANES = 128
PART = LANES - 16
AXES = ("gx", "gy", "gz")
HALF = (BOX - 1) / 2.0
VMEM_BYTES = 8 << 20
harmonic_scale = 0.5 / math.sqrt(3.0)
f32 = jnp.float32
bf16 = jnp.bfloat16
TILE = (CODES, LANES)
STATE = (2 * CODES, LANES)


def dot(a, b):
    return jnp.dot(a, b, preferred_element_type=f32)


def split(x):
    high = x.astype(bf16)
    return high, (x - high.astype(f32)).astype(bf16)


def lanes_of(shape):
    return lax.broadcasted_iota(jnp.int32, shape, len(shape) - 1)


def quotient(x, by):
    return jnp.floor((x + 0.5) * (1.0 / by))


def front(
    dims,
    cells_y,
    atom_hbm,
    corner_hbm,
    species_hbm,
    radius_hbm,
    density_hbm,
    potential_hbm,
    coulomb_hbm,
    pay_ref,
    kinds_ref,
    codes_ref,
    atom_ref,
    corner_ref,
    species_ref,
    radius_ref,
    density_ref,
    v_ref,
    c_ref,
    sems,
):
    _, ny, nz = dims
    slots = atom_ref.shape[1]
    cells, size_z = v_ref.shape
    pairs, kinds, _ = coulomb_hbm.shape
    def cut(source, target, chunks, sem):
        size = -(-source.shape[0] // chunks // 8) * 8
        for at in range(0, source.shape[0], size):
            part = slice(at, min(at + size, source.shape[0]))
            pltpu.make_async_copy(source.at[part], target.at[part], sem).start()
        return pltpu.make_async_copy(target, target, sem)

    v_copy = cut(potential_hbm, v_ref, 8, sems.at[5])
    sources = (atom_hbm, corner_hbm, species_hbm, radius_hbm, density_hbm)
    targets = (atom_ref, corner_ref, species_ref, radius_ref, density_ref)
    copies = [pltpu.make_async_copy(s, t, sems.at[i]) for i, (s, t) in enumerate(zip(sources, targets))]
    for copy in copies:
        copy.start()
    for k in range(kinds):
        pltpu.make_async_copy(coulomb_hbm.at[:, k : k + 1, :], c_ref.at[k], sems.at[6]).start()
    c_copy = pltpu.make_async_copy(c_ref, c_ref, sems.at[6])
    index_x, index_y, index_z = (lax.axis_index(a) for a in AXES)
    me = (index_x * ny + index_y) * nz + index_z
    row = lax.broadcasted_iota(jnp.int32, TILE, 0)
    lane = lanes_of(TILE)
    zero = jnp.zeros(TILE, f32)
    for copy in copies[:4]:
        copy.wait()

    zero_i = jnp.zeros(TILE, jnp.int32)
    kx, ky, kz, alive, kind_of = zero_i, zero_i, zero_i, zero, zero_i
    radius = jnp.ones(TILE, f32)
    codes = jnp.full(TILE, -1, jnp.int32)
    for s in range(slots):
        atom = atom_ref[0, s]
        kind = species_ref[atom]
        x, y, z = corner_ref[0, 0, s], corner_ref[1, 0, s], corner_ref[2, 0, s]
        code = (x >> 31 & 4) | (y >> 31 & 2) | (z >> 31 & 1)
        if s > 0:
            code = jnp.where((atom | x | y | z) == 0, -1, code)
        hit = row == code
        kx = jnp.where(hit, x, kx)
        ky = jnp.where(hit, y, ky)
        kz = jnp.where(hit, z, kz)
        radius = jnp.where(hit, radius_ref[kind], radius)
        kind_of = jnp.where(hit, kind, kind_of)
        alive = jnp.where(hit, 1.0, alive)
        codes = jnp.where(row == s, code, codes)
    kx, ky, kz = (k.astype(f32) for k in (kx, ky, kz))
    kinds_ref[...] = kind_of
    codes_ref[...] = codes

    inverse = 1.0 / radius
    line = (lane.astype(f32) - HALF) * inverse
    line = jnp.where(lane < BOX, jnp.exp(-line * line), 0.0)
    line = jnp.sum(line, axis=1, keepdims=True)
    norm = alive / (line * line * line)

    def over(x, width):
        return jnp.concatenate([x] * (width // LANES), axis=1)

    def axis_of(position, corner, width):
        offset = position - over(corner, width)
        inside = (offset >= 0.0) & (offset < BOX)
        return (offset - HALF) * over(inverse, width), inside

    cell = lanes_of((CODES, cells)).astype(f32)
    cell_x = quotient(cell, cells_y)
    u, in_x = axis_of(cell_x, kx, cells)
    v, in_y = axis_of(cell - cell_x * cells_y, ky, cells)
    e = jnp.where(in_x & in_y, jnp.exp(-(u * u + v * v)), 0.0)
    eu, ev = e * u, e * v
    weights = jnp.concatenate([e, eu, ev, eu * v, eu * u, ev * v], axis=0)
    w_high, w_low = split(weights)
    w, in_z = axis_of(lanes_of((CODES, size_z)).astype(f32), kz, size_z)
    g = jnp.where(in_z, jnp.exp(-w * w), 0.0)
    gw = g * w

    v_copy.wait()
    v_high, v_low = split(v_ref[...])
    both = dot(jnp.concatenate([w_high, w_low], axis=0), v_high)
    m = both[: 6 * CODES] + both[6 * CODES :] + dot(w_high, v_low)
    m0, mu, mv, muv, muu, mvv = (m[CODES * i : CODES * (i + 1)] for i in range(6))
    parts = [
        m0 * g,
        mu * g,
        mv * g,
        m0 * gw,
        muv * g,
        mv * gw,
        mu * gw,
        0.5 * (muu - mvv) * g,
        harmonic_scale * (2.0 * m0 * (gw * w) - (muu + mvv) * g),
    ]
    partial = zero
    for i, part in enumerate(parts):
        partial = jnp.where(lane == PART + i, jnp.sum(part, axis=1, keepdims=True), partial)
    partial = partial * norm

    copies[4].wait()
    c_copy.wait()
    p_high, p_low = split(c_ref[species_ref[me], :, 0, :] * (2.0 * density_ref[...]))
    rest = pairs - LANES
    ones = jnp.ones((16, pairs), bf16)
    contract = functools.partial(
        lax.dot_general, dimension_numbers=(((1,), (1,)), ((), ())), preferred_element_type=f32
    )
    field = contract(ones, p_high) + contract(ones, p_low)
    pay_ref[:CODES] = jnp.where(row == 0, field[:CODES, :LANES], 0.0)
    pay_ref[CODES:] = jnp.where(lane < PART, 0.0, partial)
    pay_ref[CODES : CODES + 1, :rest] = field[:1, LANES:]


def prepare(kinds_ref, delta_ref, projections_ref, out_ref, move_ref, high_ref, low_ref):
    shapes, kinds, pairs = delta_ref.shape
    projectors, slots, bands = projections_ref.shape
    out_ref[:, LANES:] = jnp.zeros((shapes * CODES, LANES), f32)
    kind = jnp.concatenate([kinds_ref[...]] * 2, axis=1)[:, :pairs]
    for i in range(shapes):
        rows = delta_ref[i]
        chosen = jnp.zeros((CODES, pairs), f32)
        for k in range(kinds):
            chosen = jnp.where(kind == k, rows[k : k + 1], chosen)
        out_ref[i * CODES : (i + 1) * CODES, :pairs] = chosen
    pair = lax.broadcasted_iota(jnp.int32, move_ref.shape, 0).astype(f32)
    row_of = quotient(pair, projectors)
    move_ref[...] = jnp.where(row_of == (lanes_of(move_ref.shape) // slots).astype(f32), 1.0, 0.0).astype(bf16)
    stack = projections_ref[...].reshape(projectors * slots, bands)
    stack = jnp.concatenate([stack, jnp.zeros((LANES - projectors * slots, bands), f32)], axis=0)
    high_ref[...], low_ref[...] = split(stack)


def merged(axis, size, pay_ref, second_ref, first_ref):
    index = lax.axis_index(AXES[axis])
    even = index % 2 == 0
    step = CODES // 2 >> axis
    row = lax.broadcasted_iota(jnp.int32, TILE, 0)
    higher = row // step % 2 == 1
    partial = lanes_of(TILE) >= PART
    add_up = partial & (index < size - 1)

    def tiles(ref):
        return ref[:CODES], ref[CODES:]

    x, a, b = tiles(pay_ref), tiles(first_ref), tiles(second_ref)
    down = [pltpu.roll(jnp.where(even, q, p), step, 0) for p, q in zip(a, b)]
    up = pltpu.roll(jnp.where(even, a[1], b[1]), CODES - step, 0)
    kept = jnp.where(add_up, x[1] + up, x[1])
    taken = jnp.where(partial, x[1] + down[1], down[1])
    return jnp.where(higher, down[0], x[0]), jnp.where(higher, taken, kept)


def merge(axis, size, pay_ref, first_ref, second_ref, out_ref):
    out_ref[:CODES], out_ref[CODES:] = merged(axis, size, pay_ref, first_ref, second_ref)


def back(
    axis,
    size,
    pay_ref,
    first_ref,
    second_ref,
    delta_ref,
    codes_ref,
    move_ref,
    high_ref,
    low_ref,
    dh_ref,
    applied_ref,
):
    projectors, slots, _ = applied_ref.shape
    pairs = dh_ref.shape[1]
    width = 2 * LANES
    head, tail = merged(axis, size, pay_ref, first_ref, second_ref)
    h = jnp.concatenate([head, jnp.where(lanes_of(TILE) < PART, tail, 0.0)], axis=1)
    for i in range(delta_ref.shape[0] // CODES):
        total = tail[:, PART + i : PART + i + 1]
        h = h + jnp.broadcast_to(total, (CODES, width)) * delta_ref[i * CODES : (i + 1) * CODES]
    dh_ref[...] = h[:1, :pairs]
    codes = jnp.concatenate([codes_ref[...]] * 2, axis=1)
    by_slot = jnp.zeros((CODES, width), f32)
    for c in range(CODES):
        by_slot = jnp.where(codes == c, h[c : c + 1], by_slot)
    pair = lanes_of((CODES, width)).astype(f32)
    column = pair - quotient(pair, projectors) * projectors
    column = jnp.where(pair < pairs, column, -1.0)
    high = by_slot.astype(bf16).astype(f32)
    blocks = -(-projectors * CODES // 16) * 2
    parts = [jnp.where(column == float(j), part, 0.0) for part in (high, by_slot - high) for j in range(blocks)]
    matrix = dot(jnp.concatenate(parts, axis=0).astype(bf16), move_ref[...])
    rows = blocks * CODES
    diagonal = lanes_of(TILE) % slots == lax.broadcasted_iota(jnp.int32, TILE, 0)
    matrix = jnp.where(jnp.concatenate([diagonal] * (2 * blocks), axis=0), matrix, 0.0).astype(bf16)
    both = dot(matrix, high_ref[...])
    out = both[:rows] + both[rows:] + dot(matrix[:rows], low_ref[...])
    applied_ref[...] = out[: projectors * slots].reshape(applied_ref.shape)


def swaps(dims, axis, odd):
    nx, ny, nz = dims
    size = dims[axis]

    def partner(at):
        i = at[axis]
        other = i ^ 1 if not odd else (i + 1 ^ 1) - 1
        if 0 <= other < size:
            return at[:axis] + (other,) + at[axis + 1 :]
        if axis == 0 and at[1] ^ 1 < ny:
            return (at[0], at[1] ^ 1, at[2])
        if axis == 1 and odd and size % 2 == 0:
            return (at[0], size - 1 - i, at[2])
        return at

    def line(at):
        return (at[0] * ny + at[1]) * nz + at[2]

    every = [(x, y, z) for x in range(nx) for y in range(ny) for z in range(nz)]
    return [(line(at), line(partner(at))) for at in every]


def exchange(x, dims, axis):
    first = lax.ppermute(x, AXES, swaps(dims, axis, False))
    second = lax.ppermute(x, AXES, swaps(dims, axis, True)) if dims[axis] > 2 else first
    return x, second, first


def local(
    potential,
    density_matrix,
    delta_table,
    coulomb,
    radius,
    atom_species,
    slot_atom,
    slot_corner,
    slot_count,
    projections,
):
    dims = tuple(lax.axis_size(a) for a in AXES)
    slots = slot_atom.shape[1]
    assert density_matrix.shape[0] == 1 and slots == CODES
    size_x, size_y, size_z = potential.shape
    pairs = density_matrix.shape[1]
    kinds, shapes, _ = delta_table.shape
    vmem, hbm = (pl.BlockSpec(memory_space=m) for m in (pltpu.VMEM, pltpu.HBM))
    params = pltpu.CompilerParams(vmem_limit_bytes=VMEM_BYTES)
    pay, kind_of, codes = pl.pallas_call(
        functools.partial(front, dims, size_y),
        out_shape=(pltpu.VMEM(STATE, f32), pltpu.VMEM(TILE, jnp.int32), pltpu.VMEM(TILE, jnp.int32)),
        in_specs=[hbm] * 7,
        out_specs=[vmem] * 3,
        scratch_shapes=[
            pltpu.SMEM(slot_atom.shape, jnp.int32),
            pltpu.SMEM(slot_corner.shape, jnp.int32),
            pltpu.SMEM(atom_species.shape, jnp.int32),
            pltpu.SMEM(radius.shape, f32),
            pltpu.VMEM((1, pairs), f32),
            pltpu.VMEM((size_x * size_y, size_z), f32),
            pltpu.VMEM((kinds, pairs, 1, pairs), f32),
            pltpu.SemaphoreType.DMA((7,)),
        ],
        compiler_params=params,
    )(
        *(
            pltpu.with_memory_space_constraint(x, pltpu.HBM)
            for x in (
                slot_atom,
                slot_corner,
                atom_species,
                radius,
                density_matrix,
                potential.reshape(size_x * size_y, size_z),
                coulomb.transpose(1, 0, 2),
            )
        )
    )
    bands = projections[0].transpose(1, 0, 2)
    delta, move, high, low = pl.pallas_call(
        prepare,
        out_shape=(
            pltpu.VMEM((shapes * CODES, 2 * LANES), f32),
            pltpu.VMEM((2 * LANES, LANES), bf16),
            pltpu.VMEM((LANES, bands.shape[2]), bf16),
            pltpu.VMEM((LANES, bands.shape[2]), bf16),
        ),
        in_specs=[vmem] * 3,
        out_specs=[vmem] * 4,
        compiler_params=params,
        cost_estimate=pl.CostEstimate(flops=500000, bytes_accessed=500000, transcendentals=0),
    )(kind_of, delta_table.transpose(1, 0, 2), bands)
    for axis in (2, 1):
        pay = pl.pallas_call(
            functools.partial(merge, axis, dims[axis]),
            out_shape=pltpu.VMEM(STATE, f32),
            in_specs=[vmem] * 3,
            out_specs=vmem,
            compiler_params=params,
        )(*exchange(pay, dims, axis))
    dh, applied = pl.pallas_call(
        functools.partial(back, 0, dims[0]),
        out_shape=(jax.ShapeDtypeStruct(density_matrix.shape, f32), jax.ShapeDtypeStruct(bands.shape, f32)),
        in_specs=[vmem] * 8,
        out_specs=[vmem] * 2,
        compiler_params=params,
    )(*exchange(pay, dims, 0), delta, codes, move, high, low)
    return dh, applied.transpose(1, 0, 2)[None]


def solution(mesh):
    return jax.shard_map(
        local,
        mesh=mesh,
        in_specs=(
            P("gx", "gy", "gz"),
            P(AXES, None),
            P(),
            P(),
            P(),
            P(),
            P(AXES, None),
            P(None, AXES, None),
            P(AXES),
            P(AXES, None, None, None),
        ),
        out_specs=(P(AXES, None), P(AXES, None, None, None)),
        check_vma=False,
    )
```

time: 16.2 us -> 15.8 us (0.975)
  other arithmetic: 0.31 us -> 0 us
    select_n x5 -> x0, other arithmetic: 0.28 us -> none  [the longest x3 0.27 us: exchange(): return jnp.where(higher, jnp.where(partial, x + down, down), kept)]
    pallas_call x2 -> x4, Pallas kernels: 1.12 us -> 1.17 us  [the longest x1 1.07 us: local(): pl.pallas_call(functools.partial(back, 0, dims[0]), out_shape=(jax.ShapeD...]
where the time goes in v3:
time: 15.8 us; the launch traced here: 15.6 us
  waiting for transfers between devices  7.24 us (46%)
  starting transfers between devices  4.89 us (31%)
  Pallas kernels  2.79 us (18%)
  between operations  0.68 us (4%)
    ppermute x3, waiting for transfers between devices, exchange(): first = lax.ppermute(x, AXES, swaps(dims, axis, False))  4.15 us
    ppermute x3, starting transfers between devices, exchange(): first = lax.ppermute(x, AXES, swaps(dims, axis, False))  3.27 us
    ppermute x2, waiting for transfers between devices, exchange(): lax.ppermute(x, AXES, swaps(dims, axis, True))  3.09 us
    ppermute x2, starting transfers between devices, exchange(): lax.ppermute(x, AXES, swaps(dims, axis, True))  1.62 us
    pallas_call x1, Pallas kernels, local(): pl.pallas_call(functools.partial(front, dims, size_y), out_shape=(pltpu.V...  1.61 us
    pallas_call x1, Pallas kernels, local(): pl.pallas_call(functools.partial(back, 0, dims[0]), out_shape=(jax.ShapeD...  1.07 us
  transfers between devices with their start and end apart: 5, of which 4 were waited for; matrix products, arithmetic and copies ran while one was open for 0% of the time, Pallas kernels for 0%

profile of v3, /device:TPU:16, one launch (start us, length us, event | category | flops | bytes accessed | tf_op | source)
XLA Modules:
  0.0 15.6 jit_solution(7206412970575068009)
XLA Ops:
  0.6 0.0 copy-start
  0.6 1.6 %shard_map.104 = (f32[16,128]{1,0:T(8,128)S(1)}, s32[8,128]{1,0:T(8,128)S(1)}, s32[8,128]{1,0:T(8,128)S(1)}) custom-call(s32[1,8]{1,0:T(1,128)} %atom_hbm.1, s32[3,1,8]{2,1,0:T(1,128)} %corner_hbm.1, s32[32]{0:T(128)} %species_hbm.1, f32[4]{0:T(128)} %radius_hbm.1, f32[1,169]{1,0:T(1,128)} %density_hbm.1, f32[768,128]{1,0:T(8,128)} %bitcast.12, ...), custom_call_target="tpu_custom_call" | custom-call | tf_op jit(solution)/shard_map/pallas_call | solution.py:309
  2.3 0.0 copy-start.1
  2.3 1.6 %collective-permute-start = (f32[16,128]{1,0:T(8,128)S(1)}, f32[16,128]{1,0:T(8,128)S(1)}, u32[]{:S(2)}, u32[]{:S(2)}) collective-permute-start(f32[16,128]{1,0:T(8,128)S(1)} %get-tuple-element.11.pay_ref), channel_id=1, source_target_pairs={{0,1},{1,0},{2,3},{3,2},{4,5},{5,4},{6,7},{7,6},{8,9},{9,8},{10,11... | collective-permute-start | bytes 24584 | tf_op jit(solution)/shard_map/ppermute | solution.py:284
  3.8 2.2 %collective-permute-done.first_ref.second_ref = f32[16,128]{1,0:T(8,128)S(1)} collective-permute-done((f32[16,128]{1,0:T(8,128)S(1)}, f32[16,128]{1,0:T(8,128)S(1)}, u32[]{:S(2)}, u32[]{:S(2)}) %collective-permute-start) | collective-permute-done | bytes 8224 | tf_op jit(solution)/shard_map/ppermute | solution.py:284
  6.0 0.1 collective-permute-start.2
  6.1 1.6 %collective-permute-start.1 = (f32[16,128]{1,0:T(8,128)S(1)}, f32[16,128]{1,0:T(8,128)S(1)}, u32[]{:S(2)}, u32[]{:S(2)}) collective-permute-start(f32[16,128]{1,0:T(8,128)S(1)} %shard_map.105.pay_ref), channel_id=1, source_target_pairs={{0,6},{1,7},{2,4},{3,5},{4,2},{5,3},{6,0},{7,1},{8,14},{9,15},{10,... | collective-permute-start | bytes 24584 | tf_op jit(solution)/shard_map/ppermute | solution.py:285
  7.7 0.0 collective-permute-done.2.second_ref
  7.7 1.5 %collective-permute-done.1.first_ref = f32[16,128]{1,0:T(8,128)S(1)} collective-permute-done((f32[16,128]{1,0:T(8,128)S(1)}, f32[16,128]{1,0:T(8,128)S(1)}, u32[]{:S(2)}, u32[]{:S(2)}) %collective-permute-start.1) | collective-permute-done | bytes 8224 | tf_op jit(solution)/shard_map/ppermute | solution.py:285
  9.2 1.6 %collective-permute-start.4 = (f32[16,128]{1,0:T(8,128)S(1)}, f32[16,128]{1,0:T(8,128)S(1)}, u32[]{:S(2)}, u32[]{:S(2)}) collective-permute-start(f32[16,128]{1,0:T(8,128)S(1)} %shard_map.106.pay_ref), channel_id=1, source_target_pairs={{0,8},{1,9},{2,10},{3,11},{4,12},{5,13},{6,14},{7,15},{8,0},{9,1},... | collective-permute-start | bytes 24584 | tf_op jit(solution)/shard_map/ppermute | solution.py:284
  10.9 0.0 collective-permute-start.3
  10.9 0.0 copy-done
  10.9 0.0 copy-done.1
  10.9 0.1 shard_map.107
  11.0 2.0 %collective-permute-done.4.second_ref = f32[16,128]{1,0:T(8,128)S(1)} collective-permute-done((f32[16,128]{1,0:T(8,128)S(1)}, f32[16,128]{1,0:T(8,128)S(1)}, u32[]{:S(2)}, u32[]{:S(2)}) %collective-permute-start.4) | collective-permute-done | bytes 8224 | tf_op jit(solution)/shard_map/ppermute | solution.py:284
  13.0 1.6 %collective-permute-done.3.first_ref = f32[16,128]{1,0:T(8,128)S(1)} collective-permute-done((f32[16,128]{1,0:T(8,128)S(1)}, f32[16,128]{1,0:T(8,128)S(1)}, u32[]{:S(2)}, u32[]{:S(2)}) %collective-permute-start.3) | collective-permute-done | bytes 8224 | tf_op jit(solution)/shard_map/ppermute | solution.py:285
  14.5 1.1 %shard_map.108 = (f32[1,169]{1,0:T(1,128)}, f32[13,8,256]{2,1,0:T(8,128)}) custom-call(f32[16,128]{1,0:T(8,128)S(1)} %shard_map.106.pay_ref, f32[16,128]{1,0:T(8,128)S(1)} %collective-permute-done.3.first_ref, f32[16,128]{1,0:T(8,128)S(1)} %collective-permute-done.4.second_ref, f32[72,256]{1,0:T(8,128)S(1)} %get-tuple-element.13.delta_ref, ...), custom_call_target="tpu_custom_call" | custom-call | tf_op jit(solution)/shard_map/pallas_call | solution.py:361
  (2 shorter events, 0.0 us)
Async XLA Ops:
  0.6 10.3 %copy-start = (f32[1,8,13,256]{3,1,2,0:T(8,128)S(1)}, f32[1,8,13,256]{3,1,2,0:T(8,128)}, u32[]{:S(2)}) copy-start(f32[1,8,13,256]{3,1,2,0:T(8,128)} %param.18) | copy-start | bytes 319492
  2.3 8.6 %copy-start.1 = (f32[4,9,169]{2,0,1:T(4,128)S(1)}, f32[4,9,169]{2,0,1:T(4,128)}, u32[]{:S(2)}) copy-start(f32[4,9,169]{2,0,1:T(4,128)} %param.12) | copy-start | bytes 73012
  2.3 3.7 %collective-permute-start = (f32[16,128]{1,0:T(8,128)S(1)}, f32[16,128]{1,0:T(8,128)S(1)}, u32[]{:S(2)}, u32[]{:S(2)}) collective-permute-start(f32[16,128]{1,0:T(8,128)S(1)} %get-tuple-element.11.pay_ref), channel_id=1, source_target_pairs={{0,1},{1,0},{2,3},{3,2},{4,5},{5,4},{6,7},{7,6},{8,9},{9,8},{10,11... | collective-permute-start | bytes 24584 | tf_op jit(solution)/shard_map/ppermute | solution.py:284
  6.0 1.7 %collective-permute-start.2 = (f32[16,128]{1,0:T(8,128)S(1)}, f32[16,128]{1,0:T(8,128)S(1)}, u32[]{:S(2)}, u32[]{:S(2)}) collective-permute-start(f32[16,128]{1,0:T(8,128)S(1)} %shard_map.105.pay_ref), channel_id=1, source_target_pairs={{0,2},{1,3},{2,0},{3,1},{4,6},{5,7},{6,4},{7,5},{8,10},{9,11},{10,... | collective-permute-start | bytes 24584 | tf_op jit(solution)/shard_map/ppermute | solution.py:284
  6.1 3.1 %collective-permute-start.1 = (f32[16,128]{1,0:T(8,128)S(1)}, f32[16,128]{1,0:T(8,128)S(1)}, u32[]{:S(2)}, u32[]{:S(2)}) collective-permute-start(f32[16,128]{1,0:T(8,128)S(1)} %shard_map.105.pay_ref), channel_id=1, source_target_pairs={{0,6},{1,7},{2,4},{3,5},{4,2},{5,3},{6,0},{7,1},{8,14},{9,15},{10,... | collective-permute-start | bytes 24584 | tf_op jit(solution)/shard_map/ppermute | solution.py:285
  9.2 3.7 %collective-permute-start.4 = (f32[16,128]{1,0:T(8,128)S(1)}, f32[16,128]{1,0:T(8,128)S(1)}, u32[]{:S(2)}, u32[]{:S(2)}) collective-permute-start(f32[16,128]{1,0:T(8,128)S(1)} %shard_map.106.pay_ref), channel_id=1, source_target_pairs={{0,8},{1,9},{2,10},{3,11},{4,12},{5,13},{6,14},{7,15},{8,0},{9,1},... | collective-permute-start | bytes 24584 | tf_op jit(solution)/shard_map/ppermute | solution.py:284
  10.9 3.7 %collective-permute-start.3 = (f32[16,128]{1,0:T(8,128)S(1)}, f32[16,128]{1,0:T(8,128)S(1)}, u32[]{:S(2)}, u32[]{:S(2)}) collective-permute-start(f32[16,128]{1,0:T(8,128)S(1)} %shard_map.106.pay_ref), channel_id=1, source_target_pairs={{0,2},{1,3},{2,0},{3,1},{4,6},{5,7},{6,4},{7,5},{8,16},{9,17},{10,... | collective-permute-start | bytes 24584 | tf_op jit(solution)/shard_map/ppermute | solution.py:285

commit v4 on v3

--- a/solution.py
+++ b/solution.py
@@ -161,19 +161,17 @@
 
     copies[4].wait()
     c_copy.wait()
-    p_high, p_low = split(c_ref[species_ref[me], :, 0, :] * (2.0 * density_ref[...]))
     rest = pairs - LANES
-    ones = jnp.ones((16, pairs), bf16)
-    contract = functools.partial(
-        lax.dot_general, dimension_numbers=(((1,), (1,)), ((), ())), preferred_element_type=f32
-    )
-    field = contract(ones, p_high) + contract(ones, p_low)
-    pay_ref[:CODES] = jnp.where(row == 0, field[:CODES, :LANES], 0.0)
-    pay_ref[CODES:] = jnp.where(lane < PART, 0.0, partial)
-    pay_ref[CODES : CODES + 1, :rest] = field[:1, LANES:]
-
-
-def prepare(kinds_ref, delta_ref, projections_ref, out_ref, move_ref, high_ref, low_ref):
+    total = jnp.sum(c_ref[species_ref[me], :, 0, :] * (2.0 * density_ref[...]), axis=1, keepdims=True)
+    square = (pairs, LANES)
+    shift = lax.broadcasted_iota(jnp.int32, square, 0) - lanes_of(square)
+    head = jnp.sum(jnp.where(shift == 0, total, 0.0), axis=0, keepdims=True)
+    tail = jnp.sum(jnp.where(shift == LANES, total, 0.0), axis=0, keepdims=True)
+    pay_ref[:CODES] = jnp.where(row == 0, head, 0.0)
+    pay_ref[CODES:] = jnp.where(lane < PART, jnp.where(row == 0, tail, 0.0), partial)
+
+
+def prepare(kinds_ref, delta_ref, projections_ref, out_ref, stack_ref):
     shapes, kinds, pairs = delta_ref.shape
     projectors, slots, bands = projections_ref.shape
     out_ref[:, LANES:] = jnp.zeros((shapes * CODES, LANES), f32)
@@ -184,12 +182,11 @@
         for k in range(kinds):
             chosen = jnp.where(kind == k, rows[k : k + 1], chosen)
         out_ref[i * CODES : (i + 1) * CODES, :pairs] = chosen
-    pair = lax.broadcasted_iota(jnp.int32, move_ref.shape, 0).astype(f32)
-    row_of = quotient(pair, projectors)
-    move_ref[...] = jnp.where(row_of == (lanes_of(move_ref.shape) // slots).astype(f32), 1.0, 0.0).astype(bf16)
     stack = projections_ref[...].reshape(projectors * slots, bands)
     stack = jnp.concatenate([stack, jnp.zeros((LANES - projectors * slots, bands), f32)], axis=0)
-    high_ref[...], low_ref[...] = split(stack)
+    high, low = split(stack)
+    for at, part in enumerate((high, high, low)):
+        stack_ref[at * LANES : (at + 1) * LANES] = part
 
 
 def merged(axis, size, pay_ref, second_ref, first_ref):
@@ -224,9 +221,7 @@
     second_ref,
     delta_ref,
     codes_ref,
-    move_ref,
-    high_ref,
-    low_ref,
+    stack_ref,
     dh_ref,
     applied_ref,
 ):
@@ -239,22 +234,21 @@
         total = tail[:, PART + i : PART + i + 1]
         h = h + jnp.broadcast_to(total, (CODES, width)) * delta_ref[i * CODES : (i + 1) * CODES]
     dh_ref[...] = h[:1, :pairs]
-    codes = jnp.concatenate([codes_ref[...]] * 2, axis=1)
-    by_slot = jnp.zeros((CODES, width), f32)
-    for c in range(CODES):
-        by_slot = jnp.where(codes == c, h[c : c + 1], by_slot)
-    pair = lanes_of((CODES, width)).astype(f32)
-    column = pair - quotient(pair, projectors) * projectors
-    column = jnp.where(pair < pairs, column, -1.0)
-    high = by_slot.astype(bf16).astype(f32)
-    blocks = -(-projectors * CODES // 16) * 2
-    parts = [jnp.where(column == float(j), part, 0.0) for part in (high, by_slot - high) for j in range(blocks)]
-    matrix = dot(jnp.concatenate(parts, axis=0).astype(bf16), move_ref[...])
-    rows = blocks * CODES
-    diagonal = lanes_of(TILE) % slots == lax.broadcasted_iota(jnp.int32, TILE, 0)
-    matrix = jnp.where(jnp.concatenate([diagonal] * (2 * blocks), axis=0), matrix, 0.0).astype(bf16)
-    both = dot(matrix, high_ref[...])
-    out = both[:rows] + both[rows:] + dot(matrix[:rows], low_ref[...])
+    codes = codes_ref[...]
+    at = jnp.maximum(codes, 0)
+    by_slot = [jnp.where(codes < 0, 0.0, jnp.take_along_axis(half, at, axis=0)) for half in (h[:, :LANES], h[:, LANES:])]
+    lane = lanes_of(TILE)
+    diagonal = lane % slots == lax.broadcasted_iota(jnp.int32, TILE, 0)
+    rows = []
+    for j in range(projectors):
+        pair = lane // slots * projectors + j
+        chosen = jnp.take_along_axis(by_slot[0], pair % LANES, axis=1)
+        chosen = jnp.where(pair < LANES, chosen, jnp.take_along_axis(by_slot[1], pair % LANES, axis=1))
+        rows.append(jnp.where(diagonal & (lane < projectors * slots), chosen, 0.0))
+    if projectors % 2:
+        rows.append(jnp.zeros(TILE, f32))
+    high, low = split(jnp.concatenate(rows, axis=0))
+    out = dot(jnp.concatenate([high, low, high], axis=1), stack_ref[...])
     applied_ref[...] = out[: projectors * slots].reshape(applied_ref.shape)
 
 
@@ -337,16 +331,14 @@
         )
     )
     bands = projections[0].transpose(1, 0, 2)
-    delta, move, high, low = pl.pallas_call(
+    delta, stack = pl.pallas_call(
         prepare,
         out_shape=(
             pltpu.VMEM((shapes * CODES, 2 * LANES), f32),
-            pltpu.VMEM((2 * LANES, LANES), bf16),
-            pltpu.VMEM((LANES, bands.shape[2]), bf16),
-            pltpu.VMEM((LANES, bands.shape[2]), bf16),
+            pltpu.VMEM((3 * LANES, bands.shape[2]), bf16),
         ),
         in_specs=[vmem] * 3,
-        out_specs=[vmem] * 4,
+        out_specs=[vmem] * 2,
         compiler_params=params,
         cost_estimate=pl.CostEstimate(flops=500000, bytes_accessed=500000, transcendentals=0),
     )(kind_of, delta_table.transpose(1, 0, 2), bands)
@@ -361,10 +353,10 @@
     dh, applied = pl.pallas_call(
         functools.partial(back, 0, dims[0]),
         out_shape=(jax.ShapeDtypeStruct(density_matrix.shape, f32), jax.ShapeDtypeStruct(bands.shape, f32)),
-        in_specs=[vmem] * 8,
+        in_specs=[vmem] * 6,
         out_specs=[vmem] * 2,
         compiler_params=params,
-    )(*exchange(pay, dims, 0), delta, codes, move, high, low)
+    )(*exchange(pay, dims, 0), delta, codes, stack)
     return dh, applied.transpose(1, 0, 2)[None]
 
 

time: 15.8 us -> 15.6 us (0.987)
  Pallas kernels: 2.79 us -> 2.63 us
where the time goes in v4:
time: 15.6 us; the launch traced here: 15.5 us
  waiting for transfers between devices  7.28 us (47%)
  starting transfers between devices  4.89 us (31%)
  Pallas kernels  2.63 us (17%)
  between operations  0.68 us (4%)
    ppermute x3, waiting for transfers between devices, exchange(): first = lax.ppermute(x, AXES, swaps(dims, axis, False))  4.18 us
    ppermute x3, starting transfers between devices, exchange(): first = lax.ppermute(x, AXES, swaps(dims, axis, False))  3.27 us
    ppermute x2, waiting for transfers between devices, exchange(): lax.ppermute(x, AXES, swaps(dims, axis, True))  3.09 us
    ppermute x2, starting transfers between devices, exchange(): lax.ppermute(x, AXES, swaps(dims, axis, True))  1.62 us
    pallas_call x1, Pallas kernels, local(): pl.pallas_call(functools.partial(front, dims, size_y), out_shape=(pltpu.V...  1.56 us
    pallas_call x1, Pallas kernels, local(): pl.pallas_call(functools.partial(back, 0, dims[0]), out_shape=(jax.ShapeD...  1 us
  transfers between devices with their start and end apart: 5, of which 4 were waited for; matrix products, arithmetic and copies ran while one was open for 0% of the time, Pallas kernels for 0%

profile of v4, /device:TPU:16, one launch (start us, length us, event | category | flops | bytes accessed | tf_op | source)
XLA Modules:
  0.0 15.5 jit_solution(12029104868829704271)
XLA Ops:
  0.6 0.0 copy-start
  0.6 1.6 %shard_map.104 = (f32[16,128]{1,0:T(8,128)S(1)}, s32[8,128]{1,0:T(8,128)S(1)}, s32[8,128]{1,0:T(8,128)S(1)}) custom-call(s32[1,8]{1,0:T(1,128)} %atom_hbm.1, s32[3,1,8]{2,1,0:T(1,128)} %corner_hbm.1, s32[32]{0:T(128)} %species_hbm.1, f32[4]{0:T(128)} %radius_hbm.1, f32[1,169]{1,0:T(1,128)} %density_hbm.1, f32[768,128]{1,0:T(8,128)} %bitcast.12, ...), custom_call_target="tpu_custom_call" | custom-call | tf_op jit(solution)/shard_map/pallas_call | solution.py:303
  2.2 0.0 copy-start.1
  2.2 1.6 %collective-permute-start = (f32[16,128]{1,0:T(8,128)S(1)}, f32[16,128]{1,0:T(8,128)S(1)}, u32[]{:S(2)}, u32[]{:S(2)}) collective-permute-start(f32[16,128]{1,0:T(8,128)S(1)} %get-tuple-element.9.pay_ref), channel_id=1, source_target_pairs={{0,1},{1,0},{2,3},{3,2},{4,5},{5,4},{6,7},{7,6},{8,9},{9,8},{10,11... | collective-permute-start | bytes 24584 | tf_op jit(solution)/shard_map/ppermute | solution.py:278
  3.8 2.2 %collective-permute-done.first_ref.second_ref = f32[16,128]{1,0:T(8,128)S(1)} collective-permute-done((f32[16,128]{1,0:T(8,128)S(1)}, f32[16,128]{1,0:T(8,128)S(1)}, u32[]{:S(2)}, u32[]{:S(2)}) %collective-permute-start) | collective-permute-done | bytes 8224 | tf_op jit(solution)/shard_map/ppermute | solution.py:278
  6.0 0.1 collective-permute-start.2
  6.0 1.6 %collective-permute-start.1 = (f32[16,128]{1,0:T(8,128)S(1)}, f32[16,128]{1,0:T(8,128)S(1)}, u32[]{:S(2)}, u32[]{:S(2)}) collective-permute-start(f32[16,128]{1,0:T(8,128)S(1)} %shard_map.105.pay_ref), channel_id=1, source_target_pairs={{0,6},{1,7},{2,4},{3,5},{4,2},{5,3},{6,0},{7,1},{8,14},{9,15},{10,... | collective-permute-start | bytes 24584 | tf_op jit(solution)/shard_map/ppermute | solution.py:279
  7.7 0.0 collective-permute-done.2.second_ref
  7.7 1.5 %collective-permute-done.1.first_ref = f32[16,128]{1,0:T(8,128)S(1)} collective-permute-done((f32[16,128]{1,0:T(8,128)S(1)}, f32[16,128]{1,0:T(8,128)S(1)}, u32[]{:S(2)}, u32[]{:S(2)}) %collective-permute-start.1) | collective-permute-done | bytes 8224 | tf_op jit(solution)/shard_map/ppermute | solution.py:279
  9.2 1.6 %collective-permute-start.4 = (f32[16,128]{1,0:T(8,128)S(1)}, f32[16,128]{1,0:T(8,128)S(1)}, u32[]{:S(2)}, u32[]{:S(2)}) collective-permute-start(f32[16,128]{1,0:T(8,128)S(1)} %shard_map.106.pay_ref), channel_id=1, source_target_pairs={{0,8},{1,9},{2,10},{3,11},{4,12},{5,13},{6,14},{7,15},{8,0},{9,1},... | collective-permute-start | bytes 24584 | tf_op jit(solution)/shard_map/ppermute | solution.py:278
  10.8 0.0 collective-permute-start.3
  10.8 0.0 copy-done
  10.8 0.0 copy-done.1
  10.9 2.0 %collective-permute-done.4.second_ref = f32[16,128]{1,0:T(8,128)S(1)} collective-permute-done((f32[16,128]{1,0:T(8,128)S(1)}, f32[16,128]{1,0:T(8,128)S(1)}, u32[]{:S(2)}, u32[]{:S(2)}) %collective-permute-start.4) | collective-permute-done | bytes 8224 | tf_op jit(solution)/shard_map/ppermute | solution.py:278
  12.9 1.6 %collective-permute-done.3.first_ref = f32[16,128]{1,0:T(8,128)S(1)} collective-permute-done((f32[16,128]{1,0:T(8,128)S(1)}, f32[16,128]{1,0:T(8,128)S(1)}, u32[]{:S(2)}, u32[]{:S(2)}) %collective-permute-start.3) | collective-permute-done | bytes 8224 | tf_op jit(solution)/shard_map/ppermute | solution.py:279
  14.5 1.0 %shard_map.108 = (f32[1,169]{1,0:T(1,128)}, f32[13,8,256]{2,1,0:T(8,128)}) custom-call(f32[16,128]{1,0:T(8,128)S(1)} %shard_map.106.pay_ref, f32[16,128]{1,0:T(8,128)S(1)} %collective-permute-done.3.first_ref, f32[16,128]{1,0:T(8,128)S(1)} %collective-permute-done.4.second_ref, f32[72,256]{1,0:T(8,128)S(1)} %get-tuple-element.11.delta_ref, ...), custom_call_target="tpu_custom_call" | custom-call | tf_op jit(solution)/shard_map/pallas_call | solution.py:353
  (3 shorter events, 0.1 us)
Async XLA Ops:
  0.6 10.2 %copy-start = (f32[1,8,13,256]{3,1,2,0:T(8,128)S(1)}, f32[1,8,13,256]{3,1,2,0:T(8,128)}, u32[]{:S(2)}) copy-start(f32[1,8,13,256]{3,1,2,0:T(8,128)} %param.18) | copy-start | bytes 319492
  2.2 8.6 %copy-start.1 = (f32[4,9,169]{2,0,1:T(4,128)S(1)}, f32[4,9,169]{2,0,1:T(4,128)}, u32[]{:S(2)}) copy-start(f32[4,9,169]{2,0,1:T(4,128)} %param.12) | copy-start | bytes 73012
  2.2 3.7 %collective-permute-start = (f32[16,128]{1,0:T(8,128)S(1)}, f32[16,128]{1,0:T(8,128)S(1)}, u32[]{:S(2)}, u32[]{:S(2)}) collective-permute-start(f32[16,128]{1,0:T(8,128)S(1)} %get-tuple-element.9.pay_ref), channel_id=1, source_target_pairs={{0,1},{1,0},{2,3},{3,2},{4,5},{5,4},{6,7},{7,6},{8,9},{9,8},{10,11... | collective-permute-start | bytes 24584 | tf_op jit(solution)/shard_map/ppermute | solution.py:278
  6.0 1.7 %collective-permute-start.2 = (f32[16,128]{1,0:T(8,128)S(1)}, f32[16,128]{1,0:T(8,128)S(1)}, u32[]{:S(2)}, u32[]{:S(2)}) collective-permute-start(f32[16,128]{1,0:T(8,128)S(1)} %shard_map.105.pay_ref), channel_id=1, source_target_pairs={{0,2},{1,3},{2,0},{3,1},{4,6},{5,7},{6,4},{7,5},{8,10},{9,11},{10,... | collective-permute-start | bytes 24584 | tf_op jit(solution)/shard_map/ppermute | solution.py:278
  6.0 3.1 %collective-permute-start.1 = (f32[16,128]{1,0:T(8,128)S(1)}, f32[16,128]{1,0:T(8,128)S(1)}, u32[]{:S(2)}, u32[]{:S(2)}) collective-permute-start(f32[16,128]{1,0:T(8,128)S(1)} %shard_map.105.pay_ref), channel_id=1, source_target_pairs={{0,6},{1,7},{2,4},{3,5},{4,2},{5,3},{6,0},{7,1},{8,14},{9,15},{10,... | collective-permute-start | bytes 24584 | tf_op jit(solution)/shard_map/ppermute | solution.py:279
  9.2 3.7 %collective-permute-start.4 = (f32[16,128]{1,0:T(8,128)S(1)}, f32[16,128]{1,0:T(8,128)S(1)}, u32[]{:S(2)}, u32[]{:S(2)}) collective-permute-start(f32[16,128]{1,0:T(8,128)S(1)} %shard_map.106.pay_ref), channel_id=1, source_target_pairs={{0,8},{1,9},{2,10},{3,11},{4,12},{5,13},{6,14},{7,15},{8,0},{9,1},... | collective-permute-start | bytes 24584 | tf_op jit(solution)/shard_map/ppermute | solution.py:278
  10.8 3.7 %collective-permute-start.3 = (f32[16,128]{1,0:T(8,128)S(1)}, f32[16,128]{1,0:T(8,128)S(1)}, u32[]{:S(2)}, u32[]{:S(2)}) collective-permute-start(f32[16,128]{1,0:T(8,128)S(1)} %shard_map.106.pay_ref), channel_id=1, source_target_pairs={{0,2},{1,3},{2,0},{3,1},{4,6},{5,7},{6,4},{7,5},{8,16},{9,17},{10,... | collective-permute-start | bytes 24584 | tf_op jit(solution)/shard_map/ppermute | solution.py:279

commit v5 on v4

--- a/solution.py
+++ b/solution.py
@@ -13,6 +13,8 @@
 LANES = 128
 PART = LANES - 16
 AXES = ("gx", "gy", "gz")
+COLOURS = (3, 2, 2)
+ORDER = {1: (0,), 2: (0, 1), 3: (0, 1, 2)}
 HALF = (BOX - 1) / 2.0
 VMEM_BYTES = 8 << 20
 harmonic_scale = 0.5 / math.sqrt(3.0)
@@ -189,46 +191,44 @@
         stack_ref[at * LANES : (at + 1) * LANES] = part
 
 
-def merged(axis, size, pay_ref, second_ref, first_ref):
+def merged(axis, size, pay_ref, *got_refs):
     index = lax.axis_index(AXES[axis])
-    even = index % 2 == 0
+    got_refs = got_refs[::-1]
+    colours = len(got_refs)
     step = CODES // 2 >> axis
     row = lax.broadcasted_iota(jnp.int32, TILE, 0)
     higher = row // step % 2 == 1
     partial = lanes_of(TILE) >= PART
     add_up = partial & (index < size - 1)
 
-    def tiles(ref):
-        return ref[:CODES], ref[CODES:]
-
-    x, a, b = tiles(pay_ref), tiles(first_ref), tiles(second_ref)
-    down = [pltpu.roll(jnp.where(even, q, p), step, 0) for p, q in zip(a, b)]
-    up = pltpu.roll(jnp.where(even, a[1], b[1]), CODES - step, 0)
-    kept = jnp.where(add_up, x[1] + up, x[1])
-    taken = jnp.where(partial, x[1] + down[1], down[1])
-    return jnp.where(higher, down[0], x[0]), jnp.where(higher, taken, kept)
-
-
-def merge(axis, size, pay_ref, first_ref, second_ref, out_ref):
-    out_ref[:CODES], out_ref[CODES:] = merged(axis, size, pay_ref, first_ref, second_ref)
-
-
-def back(
-    axis,
-    size,
-    pay_ref,
-    first_ref,
-    second_ref,
-    delta_ref,
-    codes_ref,
-    stack_ref,
-    dh_ref,
-    applied_ref,
-):
+    def of_link(link, rows):
+        got = [ref[rows] for ref in got_refs]
+        chosen = got[0]
+        for colour in range(1, colours):
+            chosen = jnp.where(link % colours == colour, got[colour], chosen)
+        return chosen
+
+    first, last = slice(0, CODES), slice(CODES, 2 * CODES)
+    below = index + colours - 1
+    down = [pltpu.roll(of_link(below, rows), step, 0) for rows in (first, last)]
+    up = pltpu.roll(of_link(index, last), CODES - step, 0)
+    x = pay_ref[last]
+    kept = jnp.where(add_up, x + up, x)
+    taken = jnp.where(partial, x + down[1], down[1])
+    return jnp.where(higher, down[0], pay_ref[first]), jnp.where(higher, taken, kept)
+
+
+def merge(axis, size, *refs):
+    out_ref = refs[-1]
+    out_ref[:CODES], out_ref[CODES:] = merged(axis, size, *refs[:-1])
+
+
+def back(axis, size, *refs):
+    *states, delta_ref, codes_ref, stack_ref, dh_ref, applied_ref = refs
     projectors, slots, _ = applied_ref.shape
     pairs = dh_ref.shape[1]
     width = 2 * LANES
-    head, tail = merged(axis, size, pay_ref, first_ref, second_ref)
+    head, tail = merged(axis, size, *states)
     h = jnp.concatenate([head, jnp.where(lanes_of(TILE) < PART, tail, 0.0)], axis=1)
     for i in range(delta_ref.shape[0] // CODES):
         total = tail[:, PART + i : PART + i + 1]
@@ -252,18 +252,18 @@
     applied_ref[...] = out[: projectors * slots].reshape(applied_ref.shape)
 
 
-def swaps(dims, axis, odd):
+def swaps(dims, axis, colour, colours):
     nx, ny, nz = dims
     size = dims[axis]
 
     def partner(at):
         i = at[axis]
-        other = i ^ 1 if not odd else (i + 1 ^ 1) - 1
-        if 0 <= other < size:
-            return at[:axis] + (other,) + at[axis + 1 :]
+        for other in (i + 1, i - 1):
+            if 0 <= other < size and min(i, other) % colours == colour:
+                return at[:axis] + (other,) + at[axis + 1 :]
         if axis == 0 and at[1] ^ 1 < ny:
             return (at[0], at[1] ^ 1, at[2])
-        if axis == 1 and odd and size % 2 == 0:
+        if axis == 1 and colours == 2 and size % 2 == 0:
             return (at[0], size - 1 - i, at[2])
         return at
 
@@ -275,9 +275,9 @@
 
 
 def exchange(x, dims, axis):
-    first = lax.ppermute(x, AXES, swaps(dims, axis, False))
-    second = lax.ppermute(x, AXES, swaps(dims, axis, True)) if dims[axis] > 2 else first
-    return x, second, first
+    colours = COLOURS[axis] if dims[axis] > 2 else 1
+    got = {c: lax.ppermute(x, AXES, swaps(dims, axis, c, colours)) for c in ORDER[colours]}
+    return [x] + [got[c] for c in reversed(range(colours))]
 
 
 def local(
@@ -346,14 +346,12 @@
         pay = pl.pallas_call(
             functools.partial(merge, axis, dims[axis]),
             out_shape=pltpu.VMEM(STATE, f32),
-            in_specs=[vmem] * 3,
             out_specs=vmem,
             compiler_params=params,
         )(*exchange(pay, dims, axis))
     dh, applied = pl.pallas_call(
         functools.partial(back, 0, dims[0]),
         out_shape=(jax.ShapeDtypeStruct(density_matrix.shape, f32), jax.ShapeDtypeStruct(bands.shape, f32)),
-        in_specs=[vmem] * 6,
         out_specs=[vmem] * 2,
         compiler_params=params,
     )(*exchange(pay, dims, 0), delta, codes, stack)

time: 15.6 us -> 15.4 us (0.987)
  the two profiles are of different devices: /device:TPU:16 before, /device:TPU:0 now
where the time goes in v5:
time: 15.4 us; the launch traced here: 15.2 us
  starting transfers between devices  7.56 us (49%)
  waiting for transfers between devices  4.37 us (28%)
  Pallas kernels  2.63 us (17%)
  between operations  0.68 us (4%)
    ppermute x6, starting transfers between devices, exchange(): lax.ppermute(x, AXES, swaps(dims, axis, c, colours))  7.56 us
    ppermute x6, waiting for transfers between devices, exchange(): lax.ppermute(x, AXES, swaps(dims, axis, c, colours))  4.37 us
    pallas_call x1, Pallas kernels, local(): pl.pallas_call(functools.partial(front, dims, size_y), out_shape=(pltpu.V...  1.56 us
    pallas_call x1, Pallas kernels, local(): pl.pallas_call(functools.partial(back, 0, dims[0]), out_shape=(jax.ShapeD...  1 us
  transfers between devices with their start and end apart: 6, of which 3 were waited for; matrix products, arithmetic and copies ran while one was open for 0% of the time, Pallas kernels for 0%

profile of v5, /device:TPU:0, one launch (start us, length us, event | category | flops | bytes accessed | tf_op | source)
XLA Modules:
  0.0 15.2 jit_solution(2693845599848062857)
XLA Ops:
  0.6 0.0 copy-start
  0.6 1.6 %shard_map.104 = (f32[16,128]{1,0:T(8,128)S(1)}, s32[8,128]{1,0:T(8,128)S(1)}, s32[8,128]{1,0:T(8,128)S(1)}) custom-call(s32[1,8]{1,0:T(1,128)} %atom_hbm.1, s32[3,1,8]{2,1,0:T(1,128)} %corner_hbm.1, s32[32]{0:T(128)} %species_hbm.1, f32[4]{0:T(128)} %radius_hbm.1, f32[1,169]{1,0:T(1,128)} %density_hbm.1, f32[768,128]{1,0:T(8,128)} %bitcast.12, ...), custom_call_target="tpu_custom_call" | custom-call | tf_op jit(solution)/shard_map/pallas_call | solution.py:303
  2.2 0.0 copy-start.1
  2.2 3.0 %collective-permute-start = (f32[16,128]{1,0:T(8,128)S(1)}, f32[16,128]{1,0:T(8,128)S(1)}, u32[]{:S(2)}, u32[]{:S(2)}) collective-permute-start(f32[16,128]{1,0:T(8,128)S(1)} %get-tuple-element.9.refs_0_), channel_id=1, source_target_pairs={{0,1},{1,0},{2,3},{3,2},{4,5},{5,4},{6,7},{7,6},{8,9},{9,8},{10,11... | collective-permute-start | bytes 24584 | tf_op jit(solution)/shard_map/ppermute | solution.py:279
  5.3 1.6 %collective-permute-done.refs_1_ = f32[16,128]{1,0:T(8,128)S(1)} collective-permute-done((f32[16,128]{1,0:T(8,128)S(1)}, f32[16,128]{1,0:T(8,128)S(1)}, u32[]{:S(2)}, u32[]{:S(2)}) %collective-permute-start) | collective-permute-done | bytes 8224 | tf_op jit(solution)/shard_map/ppermute | solution.py:279
  6.9 0.1 collective-permute-start.2
  7.0 2.1 %collective-permute-start.1 = (f32[16,128]{1,0:T(8,128)S(1)}, f32[16,128]{1,0:T(8,128)S(1)}, u32[]{:S(2)}, u32[]{:S(2)}) collective-permute-start(f32[16,128]{1,0:T(8,128)S(1)} %shard_map.105.refs_0_), channel_id=1, source_target_pairs={{0,6},{1,7},{2,4},{3,5},{4,2},{5,3},{6,0},{7,1},{8,14},{9,15},{10,... | collective-permute-start | bytes 24584 | tf_op jit(solution)/shard_map/ppermute | solution.py:279
  9.1 0.0 collective-permute-done.2.refs_2_
  9.1 1.4 %collective-permute-done.1.refs_1_ = f32[16,128]{1,0:T(8,128)S(1)} collective-permute-done((f32[16,128]{1,0:T(8,128)S(1)}, f32[16,128]{1,0:T(8,128)S(1)}, u32[]{:S(2)}, u32[]{:S(2)}) %collective-permute-start.1) | collective-permute-done | bytes 8224 | tf_op jit(solution)/shard_map/ppermute | solution.py:279
  10.5 1.8 %collective-permute-start.5 = (f32[16,128]{1,0:T(8,128)S(1)}, f32[16,128]{1,0:T(8,128)S(1)}, u32[]{:S(2)}, u32[]{:S(2)}) collective-permute-start(f32[16,128]{1,0:T(8,128)S(1)} %shard_map.106.refs_0_), channel_id=1, source_target_pairs={{0,8},{1,9},{2,10},{3,11},{4,12},{5,13},{6,14},{7,15},{8,0},{9,1},... | collective-permute-start | bytes 24584 | tf_op jit(solution)/shard_map/ppermute | solution.py:279
  12.3 0.2 collective-permute-start.4
  12.5 0.4 %collective-permute-start.3 = (f32[16,128]{1,0:T(8,128)S(1)}, f32[16,128]{1,0:T(8,128)S(1)}, u32[]{:S(2)}, u32[]{:S(2)}) collective-permute-start(f32[16,128]{1,0:T(8,128)S(1)} %shard_map.106.refs_0_), channel_id=1, source_target_pairs={{0,2},{1,3},{2,0},{3,1},{4,6},{5,7},{6,4},{7,5},{8,10},{9,11},{10,... | collective-permute-start | bytes 24584 | tf_op jit(solution)/shard_map/ppermute | solution.py:279
  12.8 0.0 copy-done
  12.8 0.0 copy-done.1
  12.9 1.4 %collective-permute-done.5.refs_3_ = f32[16,128]{1,0:T(8,128)S(1)} collective-permute-done((f32[16,128]{1,0:T(8,128)S(1)}, f32[16,128]{1,0:T(8,128)S(1)}, u32[]{:S(2)}, u32[]{:S(2)}) %collective-permute-start.5) | collective-permute-done | bytes 8224 | tf_op jit(solution)/shard_map/ppermute | solution.py:279
  14.2 0.0 collective-permute-done.4.refs_2_
  14.2 0.0 collective-permute-done.3.refs_1_
  14.2 1.0 %shard_map.108 = (f32[1,169]{1,0:T(1,128)}, f32[13,8,256]{2,1,0:T(8,128)}) custom-call(f32[16,128]{1,0:T(8,128)S(1)} %shard_map.106.refs_0_, f32[16,128]{1,0:T(8,128)S(1)} %collective-permute-done.3.refs_1_, f32[16,128]{1,0:T(8,128)S(1)} %collective-permute-done.4.refs_2_, f32[16,128]{1,0:T(8,128)S(1)} %collective-permute-done.5.refs_3_, ...), custom_call_target="tpu_custom_call" | custom-call | tf_op jit(solution)/shard_map/pallas_call | solution.py:352
  (3 shorter events, 0.1 us)
Async XLA Ops:
  0.6 12.2 %copy-start = (f32[1,8,13,256]{3,1,2,0:T(8,128)S(1)}, f32[1,8,13,256]{3,1,2,0:T(8,128)}, u32[]{:S(2)}) copy-start(f32[1,8,13,256]{3,1,2,0:T(8,128)} %param.18) | copy-start | bytes 319492
  2.2 10.6 %copy-start.1 = (f32[4,9,169]{2,0,1:T(4,128)S(1)}, f32[4,9,169]{2,0,1:T(4,128)}, u32[]{:S(2)}) copy-start(f32[4,9,169]{2,0,1:T(4,128)} %param.12) | copy-start | bytes 73012
  2.2 4.7 %collective-permute-start = (f32[16,128]{1,0:T(8,128)S(1)}, f32[16,128]{1,0:T(8,128)S(1)}, u32[]{:S(2)}, u32[]{:S(2)}) collective-permute-start(f32[16,128]{1,0:T(8,128)S(1)} %get-tuple-element.9.refs_0_), channel_id=1, source_target_pairs={{0,1},{1,0},{2,3},{3,2},{4,5},{5,4},{6,7},{7,6},{8,9},{9,8},{10,11... | collective-permute-start | bytes 24584 | tf_op jit(solution)/shard_map/ppermute | solution.py:279
  6.9 2.2 %collective-permute-start.2 = (f32[16,128]{1,0:T(8,128)S(1)}, f32[16,128]{1,0:T(8,128)S(1)}, u32[]{:S(2)}, u32[]{:S(2)}) collective-permute-start(f32[16,128]{1,0:T(8,128)S(1)} %shard_map.105.refs_0_), channel_id=1, source_target_pairs={{0,2},{1,3},{2,0},{3,1},{4,6},{5,7},{6,4},{7,5},{8,10},{9,11},{10,... | collective-permute-start | bytes 24584 | tf_op jit(solution)/shard_map/ppermute | solution.py:279
  7.0 3.5 %collective-permute-start.1 = (f32[16,128]{1,0:T(8,128)S(1)}, f32[16,128]{1,0:T(8,128)S(1)}, u32[]{:S(2)}, u32[]{:S(2)}) collective-permute-start(f32[16,128]{1,0:T(8,128)S(1)} %shard_map.105.refs_0_), channel_id=1, source_target_pairs={{0,6},{1,7},{2,4},{3,5},{4,2},{5,3},{6,0},{7,1},{8,14},{9,15},{10,... | collective-permute-start | bytes 24584 | tf_op jit(solution)/shard_map/ppermute | solution.py:279
  10.5 3.7 %collective-permute-start.5 = (f32[16,128]{1,0:T(8,128)S(1)}, f32[16,128]{1,0:T(8,128)S(1)}, u32[]{:S(2)}, u32[]{:S(2)}) collective-permute-start(f32[16,128]{1,0:T(8,128)S(1)} %shard_map.106.refs_0_), channel_id=1, source_target_pairs={{0,8},{1,9},{2,10},{3,11},{4,12},{5,13},{6,14},{7,15},{8,0},{9,1},... | collective-permute-start | bytes 24584 | tf_op jit(solution)/shard_map/ppermute | solution.py:279
  12.3 1.9 %collective-permute-start.4 = (f32[16,128]{1,0:T(8,128)S(1)}, f32[16,128]{1,0:T(8,128)S(1)}, u32[]{:S(2)}, u32[]{:S(2)}) collective-permute-start(f32[16,128]{1,0:T(8,128)S(1)} %shard_map.106.refs_0_), channel_id=1, source_target_pairs={{0,2},{1,3},{2,0},{3,1},{4,6},{5,7},{6,4},{7,5},{8,16},{9,17},{10,... | collective-permute-start | bytes 24584 | tf_op jit(solution)/shard_map/ppermute | solution.py:279
  12.5 1.8 %collective-permute-start.3 = (f32[16,128]{1,0:T(8,128)S(1)}, f32[16,128]{1,0:T(8,128)S(1)}, u32[]{:S(2)}, u32[]{:S(2)}) collective-permute-start(f32[16,128]{1,0:T(8,128)S(1)} %shard_map.106.refs_0_), channel_id=1, source_target_pairs={{0,2},{1,3},{2,0},{3,1},{4,6},{5,7},{6,4},{7,5},{8,10},{9,11},{10,... | collective-permute-start | bytes 24584 | tf_op jit(solution)/shard_map/ppermute | solution.py:279

commit v6 on v5

--- a/solution.py
+++ b/solution.py
@@ -14,7 +14,6 @@
 PART = LANES - 16
 AXES = ("gx", "gy", "gz")
 COLOURS = (3, 2, 2)
-ORDER = {1: (0,), 2: (0, 1), 3: (0, 1, 2)}
 HALF = (BOX - 1) / 2.0
 VMEM_BYTES = 8 << 20
 harmonic_scale = 0.5 / math.sqrt(3.0)
@@ -67,6 +66,7 @@
     slots = atom_ref.shape[1]
     cells, size_z = v_ref.shape
     pairs, kinds, _ = coulomb_hbm.shape
+
     def cut(source, target, chunks, sem):
         size = -(-source.shape[0] // chunks // 8) * 8
         for at in range(0, source.shape[0], size):
@@ -276,8 +276,8 @@
 
 def exchange(x, dims, axis):
     colours = COLOURS[axis] if dims[axis] > 2 else 1
-    got = {c: lax.ppermute(x, AXES, swaps(dims, axis, c, colours)) for c in ORDER[colours]}
-    return [x] + [got[c] for c in reversed(range(colours))]
+    got = [lax.ppermute(x, AXES, swaps(dims, axis, c, colours)) for c in range(colours)]
+    return [x] + got[::-1]
 
 
 def local(
@@ -342,7 +342,7 @@
         compiler_params=params,
         cost_estimate=pl.CostEstimate(flops=500000, bytes_accessed=500000, transcendentals=0),
     )(kind_of, delta_table.transpose(1, 0, 2), bands)
-    for axis in (2, 1):
+    for axis in (1, 2):
         pay = pl.pallas_call(
             functools.partial(merge, axis, dims[axis]),
             out_shape=pltpu.VMEM(STATE, f32),

time: 15.4 us -> 15.4 us (level)
  waiting for transfers between devices: 4.37 us -> 4.74 us
  starting transfers between devices: 7.56 us -> 7.19 us
    ppermute x6, waiting for transfers between devices: 4.37 us -> 4.74 us  [exchange(): lax.ppermute(x, AXES, swaps(dims, axis, c, colours))]
    ppermute x6, starting transfers between devices: 7.56 us -> 7.19 us  [exchange(): lax.ppermute(x, AXES, swaps(dims, axis, c, colours))]
where the time goes in v6:
time: 15.4 us; the launch traced here: 15.2 us
  starting transfers between devices  7.19 us (47%)
  waiting for transfers between devices  4.74 us (31%)
  Pallas kernels  2.63 us (17%)
  between operations  0.67 us (4%)
    ppermute x6, starting transfers between devices, exchange(): lax.ppermute(x, AXES, swaps(dims, axis, c, colours))  7.19 us
    ppermute x6, waiting for transfers between devices, exchange(): lax.ppermute(x, AXES, swaps(dims, axis, c, colours))  4.74 us
    pallas_call x1, Pallas kernels, local(): pl.pallas_call(functools.partial(front, dims, size_y), out_shape=(pltpu.V...  1.56 us
    pallas_call x1, Pallas kernels, local(): pl.pallas_call(functools.partial(back, 0, dims[0]), out_shape=(jax.ShapeD...  1 us
  transfers between devices with their start and end apart: 6, of which 3 were waited for; matrix products, arithmetic and copies ran while one was open for 0% of the time, Pallas kernels for 0%

profile of v6, /device:TPU:0, one launch (start us, length us, event | category | flops | bytes accessed | tf_op | source)
XLA Modules:
  0.0 15.2 jit_solution(954276766424484894)
XLA Ops:
  0.6 0.0 copy-start
  0.6 1.6 %shard_map.104 = (f32[16,128]{1,0:T(8,128)S(1)}, s32[8,128]{1,0:T(8,128)S(1)}, s32[8,128]{1,0:T(8,128)S(1)}) custom-call(s32[1,8]{1,0:T(1,128)} %atom_hbm.1, s32[3,1,8]{2,1,0:T(1,128)} %corner_hbm.1, s32[32]{0:T(128)} %species_hbm.1, f32[4]{0:T(128)} %radius_hbm.1, f32[1,169]{1,0:T(1,128)} %density_hbm.1, f32[768,128]{1,0:T(8,128)} %bitcast.12, ...), custom_call_target="tpu_custom_call" | custom-call | tf_op jit(solution)/shard_map/pallas_call | solution.py:303
  2.2 0.0 copy-start.1
  2.2 0.6 %collective-permute-start.1 = (f32[16,128]{1,0:T(8,128)S(1)}, f32[16,128]{1,0:T(8,128)S(1)}, u32[]{:S(2)}, u32[]{:S(2)}) collective-permute-start(f32[16,128]{1,0:T(8,128)S(1)} %get-tuple-element.9.refs_0_), channel_id=1, source_target_pairs={{0,2},{1,3},{2,0},{3,1},{4,6},{5,7},{6,4},{7,5},{8,10},{9,11},{10,... | collective-permute-start | bytes 24584 | tf_op jit(solution)/shard_map/ppermute | solution.py:279
  2.8 2.6 %collective-permute-start = (f32[16,128]{1,0:T(8,128)S(1)}, f32[16,128]{1,0:T(8,128)S(1)}, u32[]{:S(2)}, u32[]{:S(2)}) collective-permute-start(f32[16,128]{1,0:T(8,128)S(1)} %get-tuple-element.9.refs_0_), channel_id=1, source_target_pairs={{0,6},{1,7},{2,4},{3,5},{4,2},{5,3},{6,0},{7,1},{8,14},{9,15},{10,... | collective-permute-start | bytes 24584 | tf_op jit(solution)/shard_map/ppermute | solution.py:279
  5.4 0.0 collective-permute-done.1.refs_2_
  5.4 1.4 %collective-permute-done.refs_1_ = f32[16,128]{1,0:T(8,128)S(1)} collective-permute-done((f32[16,128]{1,0:T(8,128)S(1)}, f32[16,128]{1,0:T(8,128)S(1)}, u32[]{:S(2)}, u32[]{:S(2)}) %collective-permute-start) | collective-permute-done | bytes 8224 | tf_op jit(solution)/shard_map/ppermute | solution.py:279
  6.8 1.7 %collective-permute-start.2 = (f32[16,128]{1,0:T(8,128)S(1)}, f32[16,128]{1,0:T(8,128)S(1)}, u32[]{:S(2)}, u32[]{:S(2)}) collective-permute-start(f32[16,128]{1,0:T(8,128)S(1)} %shard_map.105.refs_0_), channel_id=1, source_target_pairs={{0,1},{1,0},{2,3},{3,2},{4,5},{5,4},{6,7},{7,6},{8,9},{9,8},{10,11... | collective-permute-start | bytes 24584 | tf_op jit(solution)/shard_map/ppermute | solution.py:279
  8.5 2.0 %collective-permute-done.2.refs_1_ = f32[16,128]{1,0:T(8,128)S(1)} collective-permute-done((f32[16,128]{1,0:T(8,128)S(1)}, f32[16,128]{1,0:T(8,128)S(1)}, u32[]{:S(2)}, u32[]{:S(2)}) %collective-permute-start.2) | collective-permute-done | bytes 8224 | tf_op jit(solution)/shard_map/ppermute | solution.py:279
  10.5 1.8 %collective-permute-start.5 = (f32[16,128]{1,0:T(8,128)S(1)}, f32[16,128]{1,0:T(8,128)S(1)}, u32[]{:S(2)}, u32[]{:S(2)}) collective-permute-start(f32[16,128]{1,0:T(8,128)S(1)} %shard_map.106.refs_0_), channel_id=1, source_target_pairs={{0,8},{1,9},{2,10},{3,11},{4,12},{5,13},{6,14},{7,15},{8,0},{9,1},... | collective-permute-start | bytes 24584 | tf_op jit(solution)/shard_map/ppermute | solution.py:279
  12.3 0.0 collective-permute-start.4
  12.3 0.5 %collective-permute-start.3 = (f32[16,128]{1,0:T(8,128)S(1)}, f32[16,128]{1,0:T(8,128)S(1)}, u32[]{:S(2)}, u32[]{:S(2)}) collective-permute-start(f32[16,128]{1,0:T(8,128)S(1)} %shard_map.106.refs_0_), channel_id=1, source_target_pairs={{0,2},{1,3},{2,0},{3,1},{4,6},{5,7},{6,4},{7,5},{8,10},{9,11},{10,... | collective-permute-start | bytes 24584 | tf_op jit(solution)/shard_map/ppermute | solution.py:279
  12.8 0.0 copy-done
  12.8 0.0 copy-done.1
  12.9 1.4 %collective-permute-done.5.refs_3_ = f32[16,128]{1,0:T(8,128)S(1)} collective-permute-done((f32[16,128]{1,0:T(8,128)S(1)}, f32[16,128]{1,0:T(8,128)S(1)}, u32[]{:S(2)}, u32[]{:S(2)}) %collective-permute-start.5) | collective-permute-done | bytes 8224 | tf_op jit(solution)/shard_map/ppermute | solution.py:279
  14.2 0.0 collective-permute-done.4.refs_2_
  14.2 0.0 collective-permute-done.3.refs_1_
  14.2 1.0 %shard_map.108 = (f32[1,169]{1,0:T(1,128)}, f32[13,8,256]{2,1,0:T(8,128)}) custom-call(f32[16,128]{1,0:T(8,128)S(1)} %shard_map.106.refs_0_, f32[16,128]{1,0:T(8,128)S(1)} %collective-permute-done.3.refs_1_, f32[16,128]{1,0:T(8,128)S(1)} %collective-permute-done.4.refs_2_, f32[16,128]{1,0:T(8,128)S(1)} %collective-permute-done.5.refs_3_, ...), custom_call_target="tpu_custom_call" | custom-call | tf_op jit(solution)/shard_map/pallas_call | solution.py:352
  (3 shorter events, 0.1 us)
Async XLA Ops:
  0.6 12.2 %copy-start = (f32[1,8,13,256]{3,1,2,0:T(8,128)S(1)}, f32[1,8,13,256]{3,1,2,0:T(8,128)}, u32[]{:S(2)}) copy-start(f32[1,8,13,256]{3,1,2,0:T(8,128)} %param.18) | copy-start | bytes 319492
  2.2 10.6 %copy-start.1 = (f32[4,9,169]{2,0,1:T(4,128)S(1)}, f32[4,9,169]{2,0,1:T(4,128)}, u32[]{:S(2)}) copy-start(f32[4,9,169]{2,0,1:T(4,128)} %param.12) | copy-start | bytes 73012
  2.2 3.2 %collective-permute-start.1 = (f32[16,128]{1,0:T(8,128)S(1)}, f32[16,128]{1,0:T(8,128)S(1)}, u32[]{:S(2)}, u32[]{:S(2)}) collective-permute-start(f32[16,128]{1,0:T(8,128)S(1)} %get-tuple-element.9.refs_0_), channel_id=1, source_target_pairs={{0,2},{1,3},{2,0},{3,1},{4,6},{5,7},{6,4},{7,5},{8,10},{9,11},{10,... | collective-permute-start | bytes 24584 | tf_op jit(solution)/shard_map/ppermute | solution.py:279
  2.8 4.0 %collective-permute-start = (f32[16,128]{1,0:T(8,128)S(1)}, f32[16,128]{1,0:T(8,128)S(1)}, u32[]{:S(2)}, u32[]{:S(2)}) collective-permute-start(f32[16,128]{1,0:T(8,128)S(1)} %get-tuple-element.9.refs_0_), channel_id=1, source_target_pairs={{0,6},{1,7},{2,4},{3,5},{4,2},{5,3},{6,0},{7,1},{8,14},{9,15},{10,... | collective-permute-start | bytes 24584 | tf_op jit(solution)/shard_map/ppermute | solution.py:279
  6.8 3.7 %collective-permute-start.2 = (f32[16,128]{1,0:T(8,128)S(1)}, f32[16,128]{1,0:T(8,128)S(1)}, u32[]{:S(2)}, u32[]{:S(2)}) collective-permute-start(f32[16,128]{1,0:T(8,128)S(1)} %shard_map.105.refs_0_), channel_id=1, source_target_pairs={{0,1},{1,0},{2,3},{3,2},{4,5},{5,4},{6,7},{7,6},{8,9},{9,8},{10,11... | collective-permute-start | bytes 24584 | tf_op jit(solution)/shard_map/ppermute | solution.py:279
  10.5 3.7 %collective-permute-start.5 = (f32[16,128]{1,0:T(8,128)S(1)}, f32[16,128]{1,0:T(8,128)S(1)}, u32[]{:S(2)}, u32[]{:S(2)}) collective-permute-start(f32[16,128]{1,0:T(8,128)S(1)} %shard_map.106.refs_0_), channel_id=1, source_target_pairs={{0,8},{1,9},{2,10},{3,11},{4,12},{5,13},{6,14},{7,15},{8,0},{9,1},... | collective-permute-start | bytes 24584 | tf_op jit(solution)/shard_map/ppermute | solution.py:279
  12.3 1.9 %collective-permute-start.4 = (f32[16,128]{1,0:T(8,128)S(1)}, f32[16,128]{1,0:T(8,128)S(1)}, u32[]{:S(2)}, u32[]{:S(2)}) collective-permute-start(f32[16,128]{1,0:T(8,128)S(1)} %shard_map.106.refs_0_), channel_id=1, source_target_pairs={{0,2},{1,3},{2,0},{3,1},{4,6},{5,7},{6,4},{7,5},{8,16},{9,17},{10,... | collective-permute-start | bytes 24584 | tf_op jit(solution)/shard_map/ppermute | solution.py:279
  12.3 1.9 %collective-permute-start.3 = (f32[16,128]{1,0:T(8,128)S(1)}, f32[16,128]{1,0:T(8,128)S(1)}, u32[]{:S(2)}, u32[]{:S(2)}) collective-permute-start(f32[16,128]{1,0:T(8,128)S(1)} %shard_map.106.refs_0_), channel_id=1, source_target_pairs={{0,2},{1,3},{2,0},{3,1},{4,6},{5,7},{6,4},{7,5},{8,10},{9,11},{10,... | collective-permute-start | bytes 24584 | tf_op jit(solution)/shard_map/ppermute | solution.py:279

commit v7 on v5

--- a/solution.py
+++ b/solution.py
@@ -74,7 +74,7 @@
             pltpu.make_async_copy(source.at[part], target.at[part], sem).start()
         return pltpu.make_async_copy(target, target, sem)
 
-    v_copy = cut(potential_hbm, v_ref, 8, sems.at[5])
+    v_copy = cut(potential_hbm, v_ref, 1, sems.at[5])
     sources = (atom_hbm, corner_hbm, species_hbm, radius_hbm, density_hbm)
     targets = (atom_ref, corner_ref, species_ref, radius_ref, density_ref)
     copies = [pltpu.make_async_copy(s, t, sems.at[i]) for i, (s, t) in enumerate(zip(sources, targets))]
@@ -342,7 +342,7 @@
         compiler_params=params,
         cost_estimate=pl.CostEstimate(flops=500000, bytes_accessed=500000, transcendentals=0),
     )(kind_of, delta_table.transpose(1, 0, 2), bands)
-    for axis in (2, 1):
+    for axis in (0, 1):
         pay = pl.pallas_call(
             functools.partial(merge, axis, dims[axis]),
             out_shape=pltpu.VMEM(STATE, f32),
@@ -350,11 +350,11 @@
             compiler_params=params,
         )(*exchange(pay, dims, axis))
     dh, applied = pl.pallas_call(
-        functools.partial(back, 0, dims[0]),
+        functools.partial(back, 2, dims[2]),
         out_shape=(jax.ShapeDtypeStruct(density_matrix.shape, f32), jax.ShapeDtypeStruct(bands.shape, f32)),
         out_specs=[vmem] * 2,
         compiler_params=params,
-    )(*exchange(pay, dims, 0), delta, codes, stack)
+    )(*exchange(pay, dims, 2), delta, codes, stack)
     return dh, applied.transpose(1, 0, 2)[None]
 
 

time: 15.4 us -> 15.4 us (level)
  no operation moved by 1% of the time
where the time goes in v7:
time: 15.4 us; the launch traced here: 15.2 us
  starting transfers between devices  7.48 us (49%)
  waiting for transfers between devices  4.45 us (29%)
  Pallas kernels  2.61 us (17%)
  between operations  0.68 us (4%)
    ppermute x6, starting transfers between devices, exchange(): lax.ppermute(x, AXES, swaps(dims, axis, c, colours))  7.48 us
    ppermute x6, waiting for transfers between devices, exchange(): lax.ppermute(x, AXES, swaps(dims, axis, c, colours))  4.45 us
    pallas_call x1, Pallas kernels, local(): pl.pallas_call(functools.partial(front, dims, size_y), out_shape=(pltpu.V...  1.55 us
    pallas_call x1, Pallas kernels, local(): pl.pallas_call(functools.partial(back, 2, dims[2]), out_shape=(jax.ShapeD...  0.98 us
  transfers between devices with their start and end apart: 6, of which 3 were waited for; matrix products, arithmetic and copies ran while one was open for 0% of the time, Pallas kernels for 0%

profile of v7, /device:TPU:0, one launch (start us, length us, event | category | flops | bytes accessed | tf_op | source)
XLA Modules:
  0.0 15.2 jit_solution(11031798808101037362)
XLA Ops:
  0.6 0.0 copy-start
  0.6 1.5 %shard_map.104 = (f32[16,128]{1,0:T(8,128)S(1)}, s32[8,128]{1,0:T(8,128)S(1)}, s32[8,128]{1,0:T(8,128)S(1)}) custom-call(s32[1,8]{1,0:T(1,128)} %atom_hbm.1, s32[3,1,8]{2,1,0:T(1,128)} %corner_hbm.1, s32[32]{0:T(128)} %species_hbm.1, f32[4]{0:T(128)} %radius_hbm.1, f32[1,169]{1,0:T(1,128)} %density_hbm.1, f32[768,128]{1,0:T(8,128)} %bitcast.12, ...), custom_call_target="tpu_custom_call" | custom-call | tf_op jit(solution)/shard_map/pallas_call | solution.py:303
  2.2 0.0 copy-start.1
  2.2 3.1 %collective-permute-start.2 = (f32[16,128]{1,0:T(8,128)S(1)}, f32[16,128]{1,0:T(8,128)S(1)}, u32[]{:S(2)}, u32[]{:S(2)}) collective-permute-start(f32[16,128]{1,0:T(8,128)S(1)} %get-tuple-element.9.refs_0_), channel_id=1, source_target_pairs={{0,8},{1,9},{2,10},{3,11},{4,12},{5,13},{6,14},{7,15},{8,0},{9,1},... | collective-permute-start | bytes 24584 | tf_op jit(solution)/shard_map/ppermute | solution.py:279
  5.3 0.0 collective-permute-start.1
  5.3 0.5 %collective-permute-start = (f32[16,128]{1,0:T(8,128)S(1)}, f32[16,128]{1,0:T(8,128)S(1)}, u32[]{:S(2)}, u32[]{:S(2)}) collective-permute-start(f32[16,128]{1,0:T(8,128)S(1)} %get-tuple-element.9.refs_0_), channel_id=1, source_target_pairs={{0,2},{1,3},{2,0},{3,1},{4,6},{5,7},{6,4},{7,5},{8,10},{9,11},{10,... | collective-permute-start | bytes 24584 | tf_op jit(solution)/shard_map/ppermute | solution.py:279
  5.8 1.1 %collective-permute-done.2.refs_3_ = f32[16,128]{1,0:T(8,128)S(1)} collective-permute-done((f32[16,128]{1,0:T(8,128)S(1)}, f32[16,128]{1,0:T(8,128)S(1)}, u32[]{:S(2)}, u32[]{:S(2)}) %collective-permute-start.2) | collective-permute-done | bytes 8224 | tf_op jit(solution)/shard_map/ppermute | solution.py:279
  7.0 0.0 collective-permute-done.1.refs_2_
  7.0 0.0 collective-permute-done.refs_1_
  7.0 0.1 collective-permute-start.4
  7.1 2.0 %collective-permute-start.3 = (f32[16,128]{1,0:T(8,128)S(1)}, f32[16,128]{1,0:T(8,128)S(1)}, u32[]{:S(2)}, u32[]{:S(2)}) collective-permute-start(f32[16,128]{1,0:T(8,128)S(1)} %shard_map.105.refs_0_), channel_id=1, source_target_pairs={{0,6},{1,7},{2,4},{3,5},{4,2},{5,3},{6,0},{7,1},{8,14},{9,15},{10,... | collective-permute-start | bytes 24584 | tf_op jit(solution)/shard_map/ppermute | solution.py:279
  9.1 0.0 collective-permute-done.4.refs_2_
  9.1 1.4 %collective-permute-done.3.refs_1_ = f32[16,128]{1,0:T(8,128)S(1)} collective-permute-done((f32[16,128]{1,0:T(8,128)S(1)}, f32[16,128]{1,0:T(8,128)S(1)}, u32[]{:S(2)}, u32[]{:S(2)}) %collective-permute-start.3) | collective-permute-done | bytes 8224 | tf_op jit(solution)/shard_map/ppermute | solution.py:279
  10.5 1.7 %collective-permute-start.5 = (f32[16,128]{1,0:T(8,128)S(1)}, f32[16,128]{1,0:T(8,128)S(1)}, u32[]{:S(2)}, u32[]{:S(2)}) collective-permute-start(f32[16,128]{1,0:T(8,128)S(1)} %shard_map.106.refs_0_), channel_id=1, source_target_pairs={{0,1},{1,0},{2,3},{3,2},{4,5},{5,4},{6,7},{7,6},{8,9},{9,8},{10,11... | collective-permute-start | bytes 24584 | tf_op jit(solution)/shard_map/ppermute | solution.py:279
  12.2 0.0 copy-done
  12.2 0.0 copy-done.1
  12.3 2.0 %collective-permute-done.5.refs_1_ = f32[16,128]{1,0:T(8,128)S(1)} collective-permute-done((f32[16,128]{1,0:T(8,128)S(1)}, f32[16,128]{1,0:T(8,128)S(1)}, u32[]{:S(2)}, u32[]{:S(2)}) %collective-permute-start.5) | collective-permute-done | bytes 8224 | tf_op jit(solution)/shard_map/ppermute | solution.py:279
  14.2 1.0 %shard_map.108 = (f32[1,169]{1,0:T(1,128)}, f32[13,8,256]{2,1,0:T(8,128)}) custom-call(f32[16,128]{1,0:T(8,128)S(1)} %shard_map.106.refs_0_, f32[16,128]{1,0:T(8,128)S(1)} %collective-permute-done.5.refs_1_, f32[72,256]{1,0:T(8,128)S(1)} %get-tuple-element.11.refs_2_, s32[8,128]{1,0:T(8,128)S(1)} %get-tuple-element.12.refs_3_, ...), custom_call_target="tpu_custom_call" | custom-call | tf_op jit(solution)/shard_map/pallas_call | solution.py:352
  (3 shorter events, 0.1 us)
Async XLA Ops:
  0.6 11.6 %copy-start = (f32[1,8,13,256]{3,1,2,0:T(8,128)S(1)}, f32[1,8,13,256]{3,1,2,0:T(8,128)}, u32[]{:S(2)}) copy-start(f32[1,8,13,256]{3,1,2,0:T(8,128)} %param.18) | copy-start | bytes 319492
  2.2 10.0 %copy-start.1 = (f32[4,9,169]{2,0,1:T(4,128)S(1)}, f32[4,9,169]{2,0,1:T(4,128)}, u32[]{:S(2)}) copy-start(f32[4,9,169]{2,0,1:T(4,128)} %param.12) | copy-start | bytes 73012
  2.2 4.7 %collective-permute-start.2 = (f32[16,128]{1,0:T(8,128)S(1)}, f32[16,128]{1,0:T(8,128)S(1)}, u32[]{:S(2)}, u32[]{:S(2)}) collective-permute-start(f32[16,128]{1,0:T(8,128)S(1)} %get-tuple-element.9.refs_0_), channel_id=1, source_target_pairs={{0,8},{1,9},{2,10},{3,11},{4,12},{5,13},{6,14},{7,15},{8,0},{9,1},... | collective-permute-start | bytes 24584 | tf_op jit(solution)/shard_map/ppermute | solution.py:279
  5.3 1.6 %collective-permute-start.1 = (f32[16,128]{1,0:T(8,128)S(1)}, f32[16,128]{1,0:T(8,128)S(1)}, u32[]{:S(2)}, u32[]{:S(2)}) collective-permute-start(f32[16,128]{1,0:T(8,128)S(1)} %get-tuple-element.9.refs_0_), channel_id=1, source_target_pairs={{0,2},{1,3},{2,0},{3,1},{4,6},{5,7},{6,4},{7,5},{8,16},{9,17},{10,... | collective-permute-start | bytes 24584 | tf_op jit(solution)/shard_map/ppermute | solution.py:279
  5.3 1.6 %collective-permute-start = (f32[16,128]{1,0:T(8,128)S(1)}, f32[16,128]{1,0:T(8,128)S(1)}, u32[]{:S(2)}, u32[]{:S(2)}) collective-permute-start(f32[16,128]{1,0:T(8,128)S(1)} %get-tuple-element.9.refs_0_), channel_id=1, source_target_pairs={{0,2},{1,3},{2,0},{3,1},{4,6},{5,7},{6,4},{7,5},{8,10},{9,11},{10,... | collective-permute-start | bytes 24584 | tf_op jit(solution)/shard_map/ppermute | solution.py:279
  7.0 2.1 %collective-permute-start.4 = (f32[16,128]{1,0:T(8,128)S(1)}, f32[16,128]{1,0:T(8,128)S(1)}, u32[]{:S(2)}, u32[]{:S(2)}) collective-permute-start(f32[16,128]{1,0:T(8,128)S(1)} %shard_map.105.refs_0_), channel_id=1, source_target_pairs={{0,2},{1,3},{2,0},{3,1},{4,6},{5,7},{6,4},{7,5},{8,10},{9,11},{10,... | collective-permute-start | bytes 24584 | tf_op jit(solution)/shard_map/ppermute | solution.py:279
  7.1 3.4 %collective-permute-start.3 = (f32[16,128]{1,0:T(8,128)S(1)}, f32[16,128]{1,0:T(8,128)S(1)}, u32[]{:S(2)}, u32[]{:S(2)}) collective-permute-start(f32[16,128]{1,0:T(8,128)S(1)} %shard_map.105.refs_0_), channel_id=1, source_target_pairs={{0,6},{1,7},{2,4},{3,5},{4,2},{5,3},{6,0},{7,1},{8,14},{9,15},{10,... | collective-permute-start | bytes 24584 | tf_op jit(solution)/shard_map/ppermute | solution.py:279
  10.5 3.7 %collective-permute-start.5 = (f32[16,128]{1,0:T(8,128)S(1)}, f32[16,128]{1,0:T(8,128)S(1)}, u32[]{:S(2)}, u32[]{:S(2)}) collective-permute-start(f32[16,128]{1,0:T(8,128)S(1)} %shard_map.106.refs_0_), channel_id=1, source_target_pairs={{0,1},{1,0},{2,3},{3,2},{4,5},{5,4},{6,7},{7,6},{8,9},{9,8},{10,11... | collective-permute-start | bytes 24584 | tf_op jit(solution)/shard_map/ppermute | solution.py:279
